TPU v7x, 32 devices: a whole 2x2x4 slice. The times are simulated.
32 devices in a mesh: dp: 8 (over z, y), expert: 4 (over x, core).
Axes of the slice: x: 2, y: 2, z: 4, core: 2. Of those that a mesh axis runs over, the one named last changes fastest.
Arguments:
- expert_ids: int32 [4096, 2], P(('dp', 'expert')), parts along dimension 0, may hold values from 0 to 1, as said below
- gate_weights: float32 [4096, 2], P(('dp', 'expert')), parts along dimension 0, may hold values from 0.2 to 1
- hidden: bfloat16 [4096, 2, 1024], P(('dp', 'expert')), parts along dimension 0, may hold values from -6 to 6
- hot_down: bfloat16 [1024, 3584], P(None, 'expert'), may hold values from -0.1875 to 0.1875
- cold_down: bfloat16 [1024, 3584], P(None, 'expert'), may hold values from -0.1875 to 0.1875
Outputs:
- mixed: bfloat16 [4096, 3584], P(('dp', 'expert')), parts along dimension 0
There are 8 independent parts, one for each index of `dp`. A program takes and returns all parts, laid end to end along the dimension named above; an argument that names none is the same for every part. Nothing has to cross between parts.
Inputs may be any that keep to these rules, and one draw needn't show every extreme that they name: `expert_ids`: each token names 2 different experts. Among the 128 tokens of one device (aligned blocks) expert 1 is named by exactly 128 tokens and no expert by more than 128; one rarely chosen expert, the same for every device, is named by exactly 128 tokens of each device.
All inputs are finite; a program needn't handle non-finite values.
Results may differ from a plain program's by a relative error of at most 0.0042.
Values may be sent and summed in bfloat16 or wider, within the bound.
No kernel may reach another device: no remote copies, remote signals or barrier semaphores. Data moves between devices by JAX's collectives and lax.ppermute only.
A program may use at most 64 MiB of HBM per device.

v0:
```python
import jax
import jax.numpy as jnp
from jax import lax
from jax.sharding import PartitionSpec as P


def body(expert_ids, gate_weights, hidden, hot_down, cold_down):
    devices = lax.axis_size("expert")
    group_size = min(4, devices)
    cold_count = devices // group_size
    experts_all = cold_count + 1
    tok_rows, top_count, hidden_width = hidden.shape
    capacity = 3 * tok_rows // 4 + tok_rows // 4 * (3 - min(experts_all, 3))
    flat_rows = tok_rows * top_count
    flat_hidden = hidden.reshape(flat_rows, hidden_width)
    flat_ids = expert_ids.reshape(flat_rows)
    hot_chosen = expert_ids == cold_count
    hot_rows = jnp.sum(
        jnp.where(hot_chosen[:, :, None], hidden, jnp.zeros((), hidden.dtype)), axis=1
    )
    hot_gate = jnp.sum(jnp.where(hot_chosen, gate_weights, jnp.zeros((), jnp.float32)), axis=1)
    hot_out = jnp.dot(
        hot_rows,
        lax.all_gather(hot_down, "expert", axis=1, tiled=True),
        preferred_element_type=jnp.float32,
    )
    hot_term = hot_gate[:, None] * hot_out
    onehot_expert = (flat_ids[None, :] == jnp.arange(cold_count, dtype=jnp.int32)[:, None]).astype(
        jnp.int32
    )
    slot_ranks = jnp.sum(onehot_expert * (jnp.cumsum(onehot_expert, axis=1) - 1), axis=0)
    slot_index = jnp.where(flat_ids < cold_count, flat_ids * capacity + slot_ranks, -1)
    placing = (
        jnp.arange(cold_count * capacity, dtype=jnp.int32)[:, None] == slot_index[None, :]
    ).astype(jnp.bfloat16)
    send_rows = jnp.dot(placing, flat_hidden, preferred_element_type=jnp.float32).astype(
        jnp.bfloat16
    )
    copies = jnp.broadcast_to(
        send_rows.reshape(cold_count, 1, capacity, hidden_width),
        (cold_count, group_size, capacity, hidden_width),
    ).reshape(devices, capacity, hidden_width)
    outputs = jnp.einsum(
        "nsf,fd->nsd",
        lax.all_to_all(copies, "expert", split_axis=0, concat_axis=0, tiled=True),
        cold_down,
        preferred_element_type=jnp.float32,
    ).astype(jnp.bfloat16)
    returned = lax.all_to_all(outputs, "expert", split_axis=0, concat_axis=0, tiled=True)
    column_blocks = returned.reshape(cold_count, group_size, capacity, -1)
    placing_blocks = placing.reshape(cold_count, capacity, flat_rows)
    row_outputs = jnp.einsum(
        "ecr,egcd->rgd", placing_blocks, column_blocks, preferred_element_type=jnp.float32
    )
    row_outputs = row_outputs.reshape(tok_rows, top_count, -1)
    scaled = row_outputs * gate_weights[:, :, None]
    cold_term = jnp.sum(scaled, axis=1)
    return (cold_term + hot_term).astype(jnp.bfloat16)


def solution(mesh):
    return jax.shard_map(
        body,
        mesh=mesh,
        in_specs=(
            P(("dp", "expert"), None),
            P(("dp", "expert"), None),
            P(("dp", "expert"), None, None),
            P(None, "expert"),
            P(None, "expert"),
        ),
        out_specs=P(("dp", "expert"), None),
        check_vma=False,
    )
```

profile of v0, /device:TPU:0, one launch (start us, length us, event | category | flops | bytes accessed | tf_op | source)
XLA Modules:
  0.0 91.6 jit_solution(15817572842629186920)
XLA Ops:
  6.5 0.7 all-gather.2.cloned.1.call-update
  7.5 0.1 reshape.155
  7.6 0.3 reduce-window.6
  7.9 0.2 slice_reduce_fusion
  8.1 0.2 reduce-window.9
  8.3 0.1 copy.9
  8.4 0.2 eq.64
  8.6 0.1 copy.7
  8.7 0.2 lt.15
  9.0 0.1 mul.34
  9.1 0.2 reshape.153
  9.4 0.2 convolution_convert_fusion
  9.8 24.4 %all_to_all.10 = bf16[4,128,1024]{2,1,0:T(8,128)(2,1)S(1)} all-to-all(bf16[4,128,1024]{2,1,0:T(8,128)(2,1)S(1)} %reshape.154), channel_id=1, replica_groups=mesh['dp'=8,'expert'=4] {'expert'}, dimensions={0} | all-to-all | bytes 2097152 | tf_op jit(solution)/shard_map/all_to_all | solution.py:45
  34.2 2.2 %fusion.5 = bf16[4,128,896]{2,1,0:T(8,128)(2,1)} fusion(bf16[4,128,1024]{2,1,0:T(8,128)(2,1)S(1)} %all_to_all.10, bf16[1024,896]{1,0:T(8,128)(2,1)S(1)} %copy-done), kind=kOutput, calls=%fused_computation.7 | convolution fusion | flops 939982848 | bytes 3801088 | tf_op jit(solution)/shard_map/nsf,fd->nsd/dot_general | solution.py:43
  36.4 3.6 %all-to-all-start.1 = ((bf16[4,128,896]{2,1,0:T(8,128)(2,1)}), bf16[4,128,896]{2,1,0:T(8,128)(2,1)S(1)}, u32[]{:S(2)}, u32[]{:S(2)}) async-start(bf16[4,128,896]{2,1,0:T(8,128)(2,1)} %fusion.5), calls=%async_computation.1 | async-start | bytes 1835008 | tf_op jit(solution)/shard_map/all_to_all | solution.py:49
  40.1 0.7 eq.68
  40.8 0.5 select_reduce_fusion
  41.3 0.1 copy.13
  41.5 1.1 %fusion.8 = bf16[128,1024]{1,0:T(8,128)(2,1)S(1)} fusion(bf16[128,2,1024]{2,1,0:T(2,128)(2,1)S(1)} %copy-done.1, pred[128,2]{1,0:T(8,128)(4,1)S(1)} %copy.13), kind=kLoop, calls=%fused_computation.10 | loop fusion | flops 393216 | bytes 786688 | tf_op jit(solution)/shard_map/reduce_sum | solution.py:18
  42.6 20.6 %all-to-all-done.1 = bf16[4,128,896]{2,1,0:T(8,128)(2,1)S(1)} async-done(((bf16[4,128,896]{2,1,0:T(8,128)(2,1)}), bf16[4,128,896]{2,1,0:T(8,128)(2,1)S(1)}, u32[]{:S(2)}, u32[]{:S(2)}) %all-to-all-start.1) | async-done | bytes 917536 | tf_op jit(solution)/shard_map/all_to_all | solution.py:49
  63.3 1.3 %copy.11 = bf16[4,896,128]{2,1,0:T(8,128)(2,1)} copy(bf16[4,896,128]{1,2,0:T(8,128)(2,1)S(1)} %bitcast.28) | data formatting | bytes 1835008 | tf_op jit(solution)/shard_map/ecr,egcd->rgd/dot_general | solution.py:52
  64.5 3.3 %fusion.4 = f32[128,3584]{1,0:T(8,128)} fusion(f32[128,2]{0,1:T(2,128)} %param.6, bf16[3584,128,1]{1,0,2:T(8,128)(2,1)} %bitcast.29, pred[128,2,128]{2,1,0:T(4,128)(4,1)S(1)} %copy-done.2), kind=kOutput, calls=%fused_computation.6 | convolution fusion | flops 236257280 | bytes 2786304 | tf_op jit(solution)/shard_map/ecr,egcd->rgd/dot_general | solution.py:52
  67.8 11.3 %all-gather.2.cloned.1.call-done = bf16[1024,3584]{1,0:T(8,128)(2,1)} async-done(((bf16[1024,896]{1,0:T(8,128)(2,1)}), bf16[1024,3584]{1,0:T(8,128)(2,1)}) %all-gather.2.cloned.1.call-update) | async-done | bytes 7340048 | tf_op jit(solution)/shard_map/all_gather | solution.py:24
  79.1 5.7 %fusion.1 = bf16[128,3584]{1,0:T(8,128)(2,1)} fusion(f32[128,3584]{1,0:T(8,128)} %fusion.4, bf16[128,1024]{1,0:T(8,128)(2,1)S(1)} %fusion.8, bf16[1024,3584]{1,0:T(8,128)(2,1)} %all-gather.2.cloned.1.call-done, f32[128]{0:T(128)S(1)} %copy-done.5), kind=kOutput, calls=%fused_computation.3 | convolution fusion | flops 940900352 | bytes 10355200 | tf_op jit(solution)/shard_map/dot_general | solution.py:22
  (22 shorter events, 0.6 us)
Async XLA Ops:
  6.5 27.6 %copy-start = (bf16[1024,896]{1,0:T(8,128)(2,1)S(1)}, bf16[1024,896]{1,0:T(8,128)(2,1)}, u32[]{:S(2)}) copy-start(bf16[1024,896]{1,0:T(8,128)(2,1)} %param.9) | copy-start | bytes 5505028
  6.5 0.8 copy-start.3
  6.5 2.6 %copy-start.1 = (bf16[128,2,1024]{2,1,0:T(2,128)(2,1)S(1)}, bf16[128,2,1024]{2,1,0:T(2,128)(2,1)}, u32[]{:S(2)}) copy-start(bf16[128,2,1024]{2,1,0:T(2,128)(2,1)} %param.7) | copy-start | bytes 1572868
  6.5 72.6 %all-gather.2.cloned.1.call-start = ((), (), s32[]{:S(2)}) async-start(), calls=%async_computation.2 | async-start | bytes 9175040 | tf_op jit(solution)/shard_map/all_gather | solution.py:24
  36.4 4.4 %copy-start.4 = (f32[128,2]{0,1:T(2,128)S(1)}, f32[128,2]{0,1:T(2,128)}, u32[]{:S(2)}) copy-start(f32[128,2]{0,1:T(2,128)} %param.6) | copy-start | bytes 3076
  36.4 26.9 %all-to-all-start.1 = ((bf16[4,128,896]{2,1,0:T(8,128)(2,1)}), bf16[4,128,896]{2,1,0:T(8,128)(2,1)S(1)}, u32[]{:S(2)}, u32[]{:S(2)}) async-start(bf16[4,128,896]{2,1,0:T(8,128)(2,1)} %fusion.5), calls=%async_computation.1 | async-start | bytes 1835008 | tf_op jit(solution)/shard_map/all_to_all | solution.py:49
  42.6 21.9 %copy-start.2 = (pred[128,2,128]{2,1,0:T(4,128)(4,1)S(1)}, pred[128,2,128]{2,1,0:T(4,128)(4,1)}, u32[]{:S(2)}) copy-start(pred[128,2,128]{2,1,0:T(4,128)(4,1)} %eq.68) | copy-start | bytes 98308
  64.5 14.6 %copy-start.5 = (f32[128]{0:T(128)S(1)}, f32[128]{0:T(128)}, u32[]{:S(2)}) copy-start(f32[128]{0:T(128)} %get-tuple-element.5) | copy-start | bytes 1540
Sparse Core Ops, SparseCore 0:
  8.9 70.1 all-gather.1
where the time goes:
time: 91.9 us; the launch traced here: 91.6 us
  waiting for transfers between devices  32.6 us (35%)
  blocking collectives  24.4 us (27%)
  between operations  13.5 us (15%)
  matrix products  11.4 us (12%)
  local copies, waits for them, and re-layouts  3.85 us (4%)
  starting transfers between devices  3.64 us (4%)
  other arithmetic  2.29 us (2%)
    all_to_all x1, blocking collectives, body(): lax.all_to_all(copies, 'expert', split_axis=0, concat_axis=0, tiled=True)  24.4 us
    all_to_all x1, waiting for transfers between devices, body(): lax.all_to_all(outputs, 'expert', split_axis=0, concat_axis=0, tiled=True)  20.6 us
    all_gather x1, waiting for transfers between devices, body(): lax.all_gather(hot_down, 'expert', axis=1, tiled=True)  11.3 us
    dot_general x1, matrix products, body(): jnp.dot(hot_rows, lax.all_gather(hot_down, 'expert', axis=1, tiled=True),...  5.66 us
    all_to_all x1, starting transfers between devices, body(): lax.all_to_all(outputs, 'expert', split_axis=0, concat_axis=0, tiled=True)  3.64 us
    dot_general x1, matrix products, body(): jnp.einsum('ecr,egcd->rgd', placing_blocks, column_blocks, preferred_elem...  3.29 us
    dot_general x1, matrix products, body(): jnp.einsum('nsf,fd->nsd', lax.all_to_all(copies, 'expert', split_axis=0,...  2.19 us
  transfers between devices with their start and end apart: 2, of which 2 were waited for; matrix products, arithmetic and copies ran while one was open for 13% of the time, Pallas kernels for 0%

commit v1 on v0

--- a/solution.py
+++ b/solution.py
@@ -4,7 +4,7 @@
 from jax.sharding import PartitionSpec as P
 
 
-def body(expert_ids, gate_weights, hidden, hot_down, cold_down):
+def general_body(expert_ids, gate_weights, hidden, hot_down, cold_down):
     devices = lax.axis_size("expert")
     group_size = min(4, devices)
     cold_count = devices // group_size
@@ -58,7 +58,59 @@
     return (cold_term + hot_term).astype(jnp.bfloat16)
 
 
+def scaled_rows(expert_ids, gate_weights, hidden):
+    parts = []
+    for expert in range(2):
+        gates = jnp.where(expert_ids == expert, gate_weights, jnp.zeros((), jnp.float32))
+        rows = jnp.sum(gates[:, :, None] * hidden.astype(jnp.float32), axis=1)
+        parts.append(rows.astype(hidden.dtype))
+    return parts
+
+
+def project(rows, weights):
+    total = jnp.dot(rows[0], weights[0], preferred_element_type=jnp.float32)
+    total += jnp.dot(rows[1], weights[1], preferred_element_type=jnp.float32)
+    return total.astype(rows[0].dtype)
+
+
+def pair_body(expert_ids, gate_weights, hidden, hot_down, cold_down):
+    devices = lax.axis_size("expert")
+    near = [(i, i ^ 1) for i in range(devices)]
+    far = [(i, i ^ 2) for i in range(devices)]
+    me = lax.axis_index("expert")
+    tok_rows = hidden.shape[0]
+    columns = hot_down.shape[1]
+    cuts = [0, tok_rows // 2, tok_rows]
+    rows = [
+        scaled_rows(expert_ids[a:b], gate_weights[a:b], hidden[a:b])
+        for a, b in zip(cuts[:-1], cuts[1:])
+    ]
+    moved = [
+        lax.ppermute(jnp.concatenate(r, axis=1), "expert", far) for r in rows
+    ]
+    own = (cold_down, hot_down)
+    partner = (lax.ppermute(cold_down, "expert", near), lax.ppermute(hot_down, "expert", near))
+    width = hidden.shape[2]
+    out = jnp.zeros((tok_rows, columns * devices), hidden.dtype)
+    mine_at, near_at = me * columns, (me ^ 1) * columns
+    far_mine_at, far_near_at = (me ^ 2) * columns, (me ^ 3) * columns
+    back = []
+    for m in moved:
+        both = (m[:, :width], m[:, width:])
+        result = jnp.concatenate([project(both, own), project(both, partner)], axis=1)
+        back.append(lax.ppermute(result, "expert", far))
+    whole = [jnp.concatenate(p, axis=0) for p in zip(*rows)]
+    out = lax.dynamic_update_slice(out, project(whole, own), (0, mine_at))
+    out = lax.dynamic_update_slice(out, project(whole, partner), (0, near_at))
+    for b, a in zip(back, cuts[:-1]):
+        out = lax.dynamic_update_slice(out, b[:, :columns], (a, far_mine_at))
+        out = lax.dynamic_update_slice(out, b[:, columns:], (a, far_near_at))
+    return out
+
+
 def solution(mesh):
+    devices = mesh.shape["expert"]
+    body = pair_body if devices == 4 else general_body
     return jax.shard_map(
         body,
         mesh=mesh,

time: 91.9 us -> 39.4 us (0.43)
  blocking collectives: 24.4 us -> 0 us
  waiting for transfers between devices: 32.6 us -> 10.8 us
  between operations: 13.5 us -> 0.17 us
  matrix products: 11.4 us -> 14.3 us
  other arithmetic: 2.29 us -> 4.85 us
  starting transfers between devices: 3.64 us -> 5.85 us
    all_to_all x1 -> x0, blocking collectives: 24.4 us -> none  [body(): lax.all_to_all(copies, 'expert', split_axis=0, concat_axis=0, tiled=True)]
    all_to_all x1 -> x0, waiting for transfers between devices: 20.6 us -> none  [body(): lax.all_to_all(outputs, 'expert', split_axis=0, concat_axis=0, tiled=True)]
    all_gather x1 -> x0, waiting for transfers between devices: 11.3 us -> none  [body(): lax.all_gather(hot_down, 'expert', axis=1, tiled=True)]
    ppermute x0 -> x6, waiting for transfers between devices: none -> 10.8 us  [the longest x2 8.84 us: pair_body(): lax.ppermute(jnp.concatenate(r, axis=1), 'expert', far)]
    ppermute x0 -> x6, starting transfers between devices: none -> 5.85 us  [the longest x2 3.2 us: pair_body(): lax.ppermute(jnp.concatenate(r, axis=1), 'expert', far)]
    all_to_all x1 -> x0, starting transfers between devices: 3.64 us -> none  [body(): lax.all_to_all(outputs, 'expert', split_axis=0, concat_axis=0, tiled=True)]
    dot_general x4 -> x12, matrix products: 11.4 us -> 14.3 us  [the longest x6 7.15 us: project(): total = jnp.dot(rows[0], weights[0], preferred_element_type=jnp.float32)]
    reduce_sum x2 -> x1, other arithmetic: 1.68 us -> 3.84 us  [scaled_rows(): rows = jnp.sum(gates[:, :, None] * hidden.astype(jnp.float32), axis=1)]
  transfers between devices with their start and end apart: 2 -> 6, of which waited for: 2 -> 3; matrix products, arithmetic and copies ran while one was open for 13% -> 32% of each run, Pallas kernels for 0% -> 0%
where the time goes in v1:
time: 39.4 us; the launch traced here: 39 us
  matrix products  14.3 us (36%)
  waiting for transfers between devices  10.8 us (27%)
  starting transfers between devices  5.85 us (15%)
  other arithmetic  4.85 us (12%)
  local copies, waits for them, and re-layouts  3.06 us (8%)
    ppermute x2, waiting for transfers between devices, pair_body(): lax.ppermute(jnp.concatenate(r, axis=1), 'expert', far)  8.84 us
    dot_general x6, matrix products, project(): total = jnp.dot(rows[0], weights[0], preferred_element_type=jnp.float32)  7.15 us
    dot_general x6, matrix products, project(): total += jnp.dot(rows[1], weights[1], preferred_element_type=jnp.float32)  7.12 us
    reduce_sum x1, other arithmetic, scaled_rows(): rows = jnp.sum(gates[:, :, None] * hidden.astype(jnp.float32), axis=1)  3.84 us
    ppermute x2, starting transfers between devices, pair_body(): lax.ppermute(jnp.concatenate(r, axis=1), 'expert', far)  3.2 us
    ppermute x2, starting transfers between devices, pair_body(): back.append(lax.ppermute(result, 'expert', far))  2.15 us
    ppermute x2, waiting for transfers between devices, pair_body(): back.append(lax.ppermute(result, 'expert', far))  2 us
    unnamed x6, local copies, waits for them, and re-layouts  1.9 us
  transfers between devices with their start and end apart: 6, of which 3 were waited for; matrix products, arithmetic and copies ran while one was open for 32% of the time, Pallas kernels for 0%

profile of v1, /device:TPU:0, one launch (start us, length us, event | category | flops | bytes accessed | tf_op | source)
XLA Modules:
  0.0 39.0 jit_solution(18307790241863039206)
XLA Ops:
  0.0 0.9 %compare_select_fusion.3 = (f32[64,2]{0,1:T(2,128)S(1)}, f32[64,2]{0,1:T(2,128)S(1)}, f32[64,2]{0,1:T(2,128)S(1)}, f32[64,2]{0,1:T(2,128)S(1)}) fusion(f32[128,2]{0,1:T(2,128)} %param.6, s32[128,2]{0,1:T(2,128)} %param.5), kind=kLoop, calls=%fused_computation.49 | loop fusion | flops 1024 | bytes 4096 | tf_op jit(solution)/shard_map/jit(_where)/select_n | solution.py:64
  1.3 3.8 %fusion.9 = (bf16[64,1024]{1,0:T(8,128)(2,1)S(1)}, bf16[64,1024]{1,0:T(8,128)(2,1)S(1)}, bf16[64,1024]{1,0:T(8,128)(2,1)S(1)}, bf16[64,1024]{1,0:T(8,128)(2,1)S(1)}) fusion(f32[64,2]{1,0:T(8,128)S(1)} %copy.8, bf16[128,2,1024]{2,1,0:T(2,128)(2,1)} %param.7, f32[64,2]{1,0:T(8,128)S(1)} %copy.9, f32[64,2]{1,0:T(8,128)S(1)} %copy.7, f32[64,2]{1,0:T(8,128)S(1)} %copy.6), kind=kLoop, calls=%fused_computation.19 | loop fusion | flops 1048576 | bytes 1050624 | tf_op jit(solution)/shard_map/reduce_sum | solution.py:65
  5.2 3.0 %collective-permute-start.4 = (bf16[64,2048]{1,0:T(8,128)(2,1)S(1)}, bf16[64,2048]{1,0:T(8,128)(2,1)S(1)}, u32[]{:S(2)}, u32[]{:S(2)}) collective-permute-start(bf16[64,2048]{1,0:T(8,128)(2,1)S(1)} %pad_maximum_fusion.3), channel_id=1, source_target_pairs={{0,2},{1,3},{2,0},{3,1},{4,6},{5,7},{6,4},{7,5},{8,10},{9,11},{10,... | collective-permute-start | bytes 786440 | tf_op jit(solution)/shard_map/ppermute | solution.py:89
  8.4 0.5 %collective-permute-start = (bf16[1024,896]{1,0:T(8,128)(2,1)S(1)}, bf16[1024,896]{1,0:T(8,128)(2,1)}, u32[]{:S(2)}, u32[]{:S(2)}) collective-permute-start(bf16[1024,896]{1,0:T(8,128)(2,1)S(1)} %copy-done), channel_id=1, source_target_pairs={{0,1},{1,0},{2,3},{3,2},{4,5},{5,4},{6,7},{7,6},{8,9},{9,8},{10,11... | collective-permute-start | bytes 5505032 | tf_op jit(solution)/shard_map/ppermute | solution.py:92
  8.9 0.4 %fusion.13 = f32[128,896]{1,0:T(8,128)S(1)} fusion(bf16[1024,896]{1,0:T(8,128)(2,1)S(1)} %copy-done, bf16[64,1024]{1,0:T(8,128)(2,1)S(1)} %get-tuple-element.7, bf16[64,1024]{1,0:T(8,128)(2,1)S(1)} %get-tuple-element.8), kind=kOutput, calls=%fused_computation.29 | convolution fusion | flops 235405312 | bytes 2555904 | tf_op jit(solution)/shard_map/dot_general | solution.py:71
  9.4 1.0 %copy-done.1 = bf16[1024,896]{1,0:T(8,128)(2,1)S(1)} copy-done((bf16[1024,896]{1,0:T(8,128)(2,1)S(1)}, bf16[1024,896]{1,0:T(8,128)(2,1)}, u32[]{:S(2)}) %copy-start.1) | copy-done | bytes 1835032
  10.4 0.5 %fusion.1 = bf16[128,3584]{1,0:T(8,128)(2,1)S(1)} fusion(bf16[128,3584]{1,0:T(8,128)(2,1)S(1)} %broadcast_in_dim.14, s32[]{:T(128)S(6)} %select_n.31, f32[128,896]{1,0:T(8,128)S(1)} %fusion.13, bf16[1024,896]{1,0:T(8,128)(2,1)S(1)} %copy-done.1, bf16[64,1024]{1,0:T(8,128)(2,1)S(1)} %get-tuple-element.6, bf16[64,1024]{1,0:T(8,128)(2,1)S(1)} %get-tuple-element.5), kind=kOutput, calls=%fused_computation.3 | convolution fusion | flops 235634688 | bytes 2785284 | tf_op jit(solution)/shard_map/dot_general | solution.py:72
  10.9 4.5 %collective-permute-done.4 = bf16[64,2048]{1,0:T(8,128)(2,1)S(1)} collective-permute-done((bf16[64,2048]{1,0:T(8,128)(2,1)S(1)}, bf16[64,2048]{1,0:T(8,128)(2,1)S(1)}, u32[]{:S(2)}, u32[]{:S(2)}) %collective-permute-start.4) | collective-permute-done | bytes 262176 | tf_op jit(solution)/shard_map/ppermute | solution.py:89
  15.4 0.4 %fusion.16 = f32[64,896]{1,0:T(8,128)S(1)} fusion(bf16[1024,896]{1,0:T(8,128)(2,1)S(1)} %copy-done.1, bf16[64,2048]{1,0:T(8,128)(2,1)S(1)} %collective-permute-done.4), kind=kOutput, calls=%fused_computation.32 | convolution fusion | flops 117440512 | bytes 2195456 | tf_op jit(solution)/shard_map/dot_general | solution.py:72
  15.8 4.3 %collective-permute-done.2 = bf16[64,2048]{1,0:T(8,128)(2,1)S(1)} collective-permute-done((bf16[64,2048]{1,0:T(8,128)(2,1)S(1)}, bf16[64,2048]{1,0:T(8,128)(2,1)S(1)}, u32[]{:S(2)}, u32[]{:S(2)}) %collective-permute-start.2) | collective-permute-done | bytes 262176 | tf_op jit(solution)/shard_map/ppermute | solution.py:89
  20.2 0.4 %fusion.22 = f32[64,896]{1,0:T(8,128)S(1)} fusion(bf16[1024,896]{1,0:T(8,128)(2,1)S(1)} %copy-done.1, bf16[64,2048]{1,0:T(8,128)(2,1)S(1)} %collective-permute-done.2), kind=kOutput, calls=%fused_computation.38 | convolution fusion | flops 117440512 | bytes 2195456 | tf_op jit(solution)/shard_map/dot_general | solution.py:72
  20.6 0.4 %fusion.6 = bf16[64,896]{1,0:T(8,128)(2,1)S(1)} fusion(f32[64,896]{1,0:T(8,128)S(1)} %fusion.16, bf16[1024,896]{1,0:T(8,128)(2,1)S(1)} %copy-done, bf16[64,2048]{1,0:T(8,128)(2,1)S(1)} %collective-permute-done.4), kind=kOutput, calls=%fused_computation.12 | convolution fusion | flops 117555200 | bytes 2310144 | tf_op jit(solution)/shard_map/dot_general | solution.py:71
  21.0 0.4 %fusion.4 = bf16[64,896]{1,0:T(8,128)(2,1)S(1)} fusion(f32[64,896]{1,0:T(8,128)S(1)} %fusion.22, bf16[1024,896]{1,0:T(8,128)(2,1)S(1)} %copy-done, bf16[64,2048]{1,0:T(8,128)(2,1)S(1)} %collective-permute-done.2), kind=kOutput, calls=%fused_computation.10 | convolution fusion | flops 117555200 | bytes 2310144 | tf_op jit(solution)/shard_map/dot_general | solution.py:71
  21.5 1.9 %fusion.14 = f32[64,896]{1,0:T(8,128)S(1)} fusion(bf16[1024,896]{1,0:T(8,128)(2,1)} %collective-permute-done.1, bf16[64,2048]{1,0:T(8,128)(2,1)S(1)} %collective-permute-done.4), kind=kOutput, calls=%fused_computation.30 | convolution fusion | flops 117440512 | bytes 2195456 | tf_op jit(solution)/shard_map/dot_general | solution.py:72
  23.4 1.9 %fusion.7 = bf16[64,896]{1,0:T(8,128)(2,1)S(1)} fusion(f32[64,896]{1,0:T(8,128)S(1)} %fusion.14, bf16[1024,896]{1,0:T(8,128)(2,1)} %collective-permute-done, bf16[64,2048]{1,0:T(8,128)(2,1)S(1)} %collective-permute-done.4), kind=kOutput, calls=%fused_computation.13 | convolution fusion | flops 117555200 | bytes 2310144 | tf_op jit(solution)/shard_map/dot_general | solution.py:71
  25.4 1.8 %collective-permute-start.5 = (bf16[64,1792]{1,0:T(8,128)(2,1)S(1)}, bf16[64,1792]{1,0:T(8,128)(2,1)S(1)}, u32[]{:S(2)}, u32[]{:S(2)}) collective-permute-start(bf16[64,1792]{1,0:T(8,128)(2,1)S(1)} %pad_maximum_fusion.5), channel_id=1, source_target_pairs={{0,2},{1,3},{2,0},{3,1},{4,6},{5,7},{6,4},{7,5},{8,10},{9,11},{10,... | collective-permute-start | bytes 688136 | tf_op jit(solution)/shard_map/ppermute | solution.py:101
  27.2 1.9 %fusion.20 = f32[64,896]{1,0:T(8,128)S(1)} fusion(bf16[1024,896]{1,0:T(8,128)(2,1)} %collective-permute-done.1, bf16[64,2048]{1,0:T(8,128)(2,1)S(1)} %collective-permute-done.2), kind=kOutput, calls=%fused_computation.36 | convolution fusion | flops 117440512 | bytes 2195456 | tf_op jit(solution)/shard_map/dot_general | solution.py:72
  29.1 1.9 %fusion.5 = bf16[64,896]{1,0:T(8,128)(2,1)S(1)} fusion(f32[64,896]{1,0:T(8,128)S(1)} %fusion.20, bf16[1024,896]{1,0:T(8,128)(2,1)} %collective-permute-done, bf16[64,2048]{1,0:T(8,128)(2,1)S(1)} %collective-permute-done.2), kind=kOutput, calls=%fused_computation.11 | convolution fusion | flops 117555200 | bytes 2310144 | tf_op jit(solution)/shard_map/dot_general | solution.py:71
  31.1 0.3 collective-permute-start.3
  31.4 1.9 %fusion.12 = f32[128,896]{1,0:T(8,128)S(1)} fusion(bf16[1024,896]{1,0:T(8,128)(2,1)} %collective-permute-done.1, bf16[64,1024]{1,0:T(8,128)(2,1)S(1)} %get-tuple-element.6, bf16[64,1024]{1,0:T(8,128)(2,1)S(1)} %get-tuple-element.5), kind=kOutput, calls=%fused_computation.28 | convolution fusion | flops 235405312 | bytes 2555904 | tf_op jit(solution)/shard_map/dot_general | solution.py:72
  33.4 2.0 %fusion.3 = bf16[128,3584]{1,0:T(8,128)(2,1)S(1)} fusion(bf16[128,3584]{1,0:T(8,128)(2,1)S(1)} %fusion.1, s32[]{:T(128)S(6)} %select_n.32, f32[128,896]{1,0:T(8,128)S(1)} %fusion.12, bf16[1024,896]{1,0:T(8,128)(2,1)} %collective-permute-done, bf16[64,1024]{1,0:T(8,128)(2,1)S(1)} %get-tuple-element.7, bf16[64,1024]{1,0:T(8,128)(2,1)S(1)} %get-tuple-element.8), kind=kOutput, calls=%fused_computation.5 | convolution fusion | flops 235634688 | bytes 2785284 | tf_op jit(solution)/shard_map/dot_general | solution.py:71
  35.4 2.0 %collective-permute-done.3 = bf16[64,1792]{1,0:T(8,128)(2,1)S(1)} collective-permute-done((bf16[64,1792]{1,0:T(8,128)(2,1)S(1)}, bf16[64,1792]{1,0:T(8,128)(2,1)S(1)}, u32[]{:S(2)}, u32[]{:S(2)}) %collective-permute-start.3) | collective-permute-done | bytes 229408 | tf_op jit(solution)/shard_map/ppermute | solution.py:101
  37.5 0.9 %copy-done.2 = bf16[128,3584]{1,0:T(8,128)(2,1)} copy-done((bf16[128,3584]{1,0:T(8,128)(2,1)}, bf16[128,3584]{1,0:T(8,128)(2,1)S(1)}, u32[]{:S(2)}) %copy-start.2) | copy-done | bytes 917528
  38.4 0.7 %slice_dynamic-update-slice_fusion = bf16[128,3584]{1,0:T(8,128)(2,1)} fusion(bf16[128,3584]{1,0:T(8,128)(2,1)} %copy-done.2, s32[]{:T(128)S(6)} %select_n.34, bf16[64,1792]{1,0:T(8,128)(2,1)S(1)} %collective-permute-done.5), kind=kLoop, calls=%fused_computation.42 | loop fusion | bytes 229380 | tf_op jit(solution)/shard_map/dynamic_update_slice | solution.py:107
  (21 shorter events, 0.8 us)
Async XLA Ops:
  0.0 8.4 %copy-start = (bf16[1024,896]{1,0:T(8,128)(2,1)S(1)}, bf16[1024,896]{1,0:T(8,128)(2,1)}, u32[]{:S(2)}) copy-start(bf16[1024,896]{1,0:T(8,128)(2,1)} %param.9) | copy-start | bytes 5505028
  5.2 10.2 %collective-permute-start.4 = (bf16[64,2048]{1,0:T(8,128)(2,1)S(1)}, bf16[64,2048]{1,0:T(8,128)(2,1)S(1)}, u32[]{:S(2)}, u32[]{:S(2)}) collective-permute-start(bf16[64,2048]{1,0:T(8,128)(2,1)S(1)} %pad_maximum_fusion.3), channel_id=1, source_target_pairs={{0,2},{1,3},{2,0},{3,1},{4,6},{5,7},{6,4},{7,5},{8,10},{9,11},{10,... | collective-permute-start | bytes 786440 | tf_op jit(solution)/shard_map/ppermute | solution.py:89
  8.2 13.2 %collective-permute-start.1 = (bf16[1024,896]{1,0:T(8,128)(2,1)}, bf16[1024,896]{1,0:T(8,128)(2,1)}, u32[]{:S(2)}, u32[]{:S(2)}) collective-permute-start(bf16[1024,896]{1,0:T(8,128)(2,1)} %param.8), channel_id=1, source_target_pairs={{0,1},{1,0},{2,3},{3,2},{4,5},{5,4},{6,7},{7,6},{8,9},{9,8},{10,11... | collective-permute-start | bytes 5505032 | tf_op jit(solution)/shard_map/ppermute | solution.py:92
  8.3 11.9 %collective-permute-start.2 = (bf16[64,2048]{1,0:T(8,128)(2,1)S(1)}, bf16[64,2048]{1,0:T(8,128)(2,1)S(1)}, u32[]{:S(2)}, u32[]{:S(2)}) collective-permute-start(bf16[64,2048]{1,0:T(8,128)(2,1)S(1)} %pad_maximum_fusion.2), channel_id=1, source_target_pairs={{0,2},{1,3},{2,0},{3,1},{4,6},{5,7},{6,4},{7,5},{8,10},{9,11},{10,... | collective-permute-start | bytes 786440 | tf_op jit(solution)/shard_map/ppermute | solution.py:89
  8.4 15.0 %collective-permute-start = (bf16[1024,896]{1,0:T(8,128)(2,1)S(1)}, bf16[1024,896]{1,0:T(8,128)(2,1)}, u32[]{:S(2)}, u32[]{:S(2)}) collective-permute-start(bf16[1024,896]{1,0:T(8,128)(2,1)S(1)} %copy-done), channel_id=1, source_target_pairs={{0,1},{1,0},{2,3},{3,2},{4,5},{5,4},{6,7},{7,6},{8,9},{9,8},{10,11... | collective-permute-start | bytes 5505032 | tf_op jit(solution)/shard_map/ppermute | solution.py:92
  8.9 1.5 %copy-start.1 = (bf16[1024,896]{1,0:T(8,128)(2,1)S(1)}, bf16[1024,896]{1,0:T(8,128)(2,1)}, u32[]{:S(2)}) copy-start(bf16[1024,896]{1,0:T(8,128)(2,1)} %param.8) | copy-start | bytes 5505028
  25.4 12.0 %collective-permute-start.5 = (bf16[64,1792]{1,0:T(8,128)(2,1)S(1)}, bf16[64,1792]{1,0:T(8,128)(2,1)S(1)}, u32[]{:S(2)}, u32[]{:S(2)}) collective-permute-start(bf16[64,1792]{1,0:T(8,128)(2,1)S(1)} %pad_maximum_fusion.5), channel_id=1, source_target_pairs={{0,2},{1,3},{2,0},{3,1},{4,6},{5,7},{6,4},{7,5},{8,10},{9,11},{10,... | collective-permute-start | bytes 688136 | tf_op jit(solution)/shard_map/ppermute | solution.py:101
  31.1 6.3 %collective-permute-start.3 = (bf16[64,1792]{1,0:T(8,128)(2,1)S(1)}, bf16[64,1792]{1,0:T(8,128)(2,1)S(1)}, u32[]{:S(2)}, u32[]{:S(2)}) collective-permute-start(bf16[64,1792]{1,0:T(8,128)(2,1)S(1)} %pad_maximum_fusion.4), channel_id=1, source_target_pairs={{0,2},{1,3},{2,0},{3,1},{4,6},{5,7},{6,4},{7,5},{8,10},{9,11},{10,... | collective-permute-start | bytes 688136 | tf_op jit(solution)/shard_map/ppermute | solution.py:101
  37.5 0.9 %copy-start.2 = (bf16[128,3584]{1,0:T(8,128)(2,1)}, bf16[128,3584]{1,0:T(8,128)(2,1)S(1)}, u32[]{:S(2)}) copy-start(bf16[128,3584]{1,0:T(8,128)(2,1)S(1)} %slice_dynamic-update-slice_fusion.1) | copy-start | bytes 2752516

commit v2 on v0

--- a/solution.py
+++ b/solution.py
@@ -1,10 +1,19 @@
+import functools
+
 import jax
 import jax.numpy as jnp
 from jax import lax
+from jax.experimental import pallas as pl
+from jax.experimental.pallas import tpu as pltpu
 from jax.sharding import PartitionSpec as P
 
-
-def body(expert_ids, gate_weights, hidden, hot_down, cold_down):
+VMEM = pl.BlockSpec(memory_space=pltpu.VMEM)
+ANY = pl.BlockSpec(memory_space=pl.ANY)
+SLAB = 128
+CUTS = (0, 5, 11, 16)
+
+
+def general_body(expert_ids, gate_weights, hidden, hot_down, cold_down):
     devices = lax.axis_size("expert")
     group_size = min(4, devices)
     cold_count = devices // group_size
@@ -58,17 +67,263 @@
     return (cold_term + hot_term).astype(jnp.bfloat16)
 
 
+def near_core(*arrays):
+    return [pltpu.with_memory_space_constraint(a, pltpu.VMEM) for a in arrays]
+
+
+def in_hbm(*arrays):
+    return [pltpu.with_memory_space_constraint(a, pltpu.HBM) for a in arrays]
+
+
+def limit(mib):
+    return pltpu.CompilerParams(vmem_limit_bytes=mib << 20)
+
+
+def rows_of(hidden_ref, start, rows_ref, sem):
+    flat = hidden_ref.reshape(hidden_ref.shape[0] * hidden_ref.shape[1], hidden_ref.shape[2])
+    return pltpu.make_async_copy(flat.at[pl.ds(start, rows_ref.shape[0])], rows_ref, sem)
+
+
+def take_kernel(start, hidden_ref, rows_ref, sems):
+    copy = rows_of(hidden_ref, start, rows_ref, sems.at[0])
+    copy.start()
+    copy.wait()
+
+
+def first_take_kernel(start, hidden_ref, ids_ref, weights_ref, rows_ref, gates_ref, ids, weights, sems):
+    copies = [
+        rows_of(hidden_ref, start, rows_ref, sems.at[0]),
+        pltpu.make_async_copy(ids_ref, ids, sems.at[1]),
+        pltpu.make_async_copy(weights_ref, weights, sems.at[2]),
+    ]
+    for copy in copies:
+        copy.start()
+    for copy in copies[1:]:
+        copy.wait()
+    for e in range(2):
+        gates_ref[2 * e : 2 * e + 2, :] = jnp.where(ids[...] == e, weights[...], 0.0)
+    copies[0].wait()
+
+
+def take(hidden, start, tokens, choice=()):
+    _, choices, depth = hidden.shape
+    shapes = [pltpu.VMEM((tokens * choices, depth), hidden.dtype)]
+    scratch = [pltpu.SemaphoreType.DMA((3,))]
+    if choice:
+        shapes.append(pltpu.VMEM((2 * choices, hidden.shape[0]), choice[1].dtype))
+        scratch = [pltpu.VMEM(c.shape, c.dtype) for c in choice] + scratch
+    return pl.pallas_call(
+        functools.partial(first_take_kernel if choice else take_kernel, start * choices),
+        name="take",
+        out_shape=shapes,
+        in_specs=[ANY] * (1 + len(choice)),
+        out_specs=[VMEM] * len(shapes),
+        scratch_shapes=scratch,
+        compiler_params=limit(2),
+        cost_estimate=pl.CostEstimate(flops=0, bytes_accessed=4 * tokens * choices * depth, transcendentals=0),
+    )(*in_hbm(hidden, *choice))
+
+
+def choose(rows, gates):
+    tokens = gates.shape[0]
+    first = 2 * lax.broadcasted_iota(jnp.int32, (tokens, 2 * tokens), 0)
+    column = lax.broadcasted_iota(jnp.int32, (tokens, 2 * tokens), 1)
+    chosen, scales = [], []
+    for expert in range(2):
+        low, high = gates[:, 2 * expert : 2 * expert + 1], gates[:, 2 * expert + 1 : 2 * expert + 2]
+        pick = (column == first + jnp.where(high != 0, 1, 0)).astype(rows.dtype)
+        picked = jnp.dot(pick, rows, preferred_element_type=jnp.float32)
+        chosen.append(picked.astype(rows.dtype))
+        scales.append(low + high)
+    return chosen, scales
+
+
+def columns_of(gates_ref):
+    return jnp.transpose(jnp.concatenate([gates_ref[...]] * 2, axis=0))
+
+
+def gated(chosen, scales, weights):
+    width = weights[0].shape[1]
+    for at in range(0, width, SLAB):
+        end = min(at + SLAB, width)
+        terms = [
+            scale * jnp.dot(x, w[:, at:end], preferred_element_type=jnp.float32)
+            for scale, x, w in zip(scales, chosen, weights)
+        ]
+        yield at, end, terms[0] + terms[1]
+
+
+def far_kernel(start, rows_ref, gates_ref, c0, h0, c1, h1, out_ref):
+    tokens, width = out_ref.shape[0], c0.shape[1]
+    chosen, scales = choose(rows_ref[...], columns_of(gates_ref)[start : start + tokens, :])
+    for i, weights in enumerate(((c0, h0), (c1, h1))):
+        for at, end, block in gated(chosen, scales, weights):
+            out_ref[:, i * width + at : i * width + end] = block.astype(out_ref.dtype)
+
+
+def cost_of(rows, width):
+    return pl.CostEstimate(
+        flops=4 * rows.shape[0] * rows.shape[1] * width, bytes_accessed=8 * rows.shape[0] * width, transcendentals=0
+    )
+
+
+def far_project(start, tokens, rows, gates, own, partner):
+    width = own[0].shape[1]
+    return pl.pallas_call(
+        functools.partial(far_kernel, start),
+        name="far_project",
+        out_shape=pltpu.VMEM((tokens, 2 * width), rows.dtype),
+        in_specs=[VMEM] * 6,
+        out_specs=VMEM,
+        compiler_params=limit(12),
+        cost_estimate=cost_of(rows, width),
+    )(*near_core(rows, gates, *own, *partner))
+
+
+def own_kernel(*refs):
+    *row_refs, gates_ref, c0, h0, c1, h1, out_ref, staged, sems = refs
+    width = c0.shape[1]
+    me = lax.axis_index("expert")
+    gates = columns_of(gates_ref)
+    chosen, scales, at = [], [], 0
+    for rows_ref in row_refs:
+        tokens = rows_ref.shape[0] // 2
+        x, g = choose(rows_ref[...], gates[at : at + tokens, :])
+        chosen.append(x)
+        scales.append(g)
+        at += tokens
+    chosen = [jnp.concatenate(x, axis=0) for x in zip(*chosen)]
+    scales = [jnp.concatenate(g, axis=0) for g in zip(*scales)]
+    copies = []
+    for i, weights in enumerate(((c0, h0), (c1, h1))):
+        for at, end, block in gated(chosen, scales, weights):
+            staged[i, :, at:end] = block.astype(staged.dtype)
+        to = pl.multiple_of((me ^ i) * width, width)
+        copies.append(pltpu.make_async_copy(staged.at[i], out_ref.at[:, pl.ds(to, width)], sems.at[i]))
+        copies[-1].start()
+    for copy in copies:
+        copy.wait()
+
+
+def own_project(devices, rows, gates, own, partner):
+    width = own[0].shape[1]
+    tokens = sum(r.shape[0] for r in rows) // 2
+    return pl.pallas_call(
+        own_kernel,
+        name="own_project",
+        out_shape=pltpu.HBM((tokens, devices * width), rows[0].dtype),
+        in_specs=[VMEM] * (len(rows) + 5),
+        out_specs=ANY,
+        scratch_shapes=[pltpu.VMEM((2, tokens, width), rows[0].dtype), pltpu.SemaphoreType.DMA((2,))],
+        compiler_params=limit(12),
+        cost_estimate=cost_of(rows[0], len(rows) * width),
+    )(*near_core(*rows, gates, *own, *partner))
+
+
+def put_kernel(start, block_ref, whole_ref, out_ref, sems):
+    del whole_ref
+    tokens, width = block_ref.shape[0], block_ref.shape[1] // 2
+    me = lax.axis_index("expert")
+    copies = []
+    for i in range(2):
+        to = pl.multiple_of((me ^ 2 ^ i) * width, width)
+        copies.append(
+            pltpu.make_async_copy(
+                block_ref.at[:, pl.ds(i * width, width)],
+                out_ref.at[pl.ds(start, tokens), pl.ds(to, width)],
+                sems.at[i],
+            )
+        )
+        copies[-1].start()
+    for copy in copies:
+        copy.wait()
+
+
+def put(start, block, whole):
+    return pl.pallas_call(
+        functools.partial(put_kernel, start),
+        name="put",
+        out_shape=pltpu.HBM(whole.shape, whole.dtype),
+        in_specs=[VMEM, ANY],
+        out_specs=ANY,
+        scratch_shapes=[pltpu.SemaphoreType.DMA((2,))],
+        input_output_aliases={1: 0},
+        compiler_params=limit(2),
+        cost_estimate=pl.CostEstimate(flops=0, bytes_accessed=4 * block.size, transcendentals=0),
+    )(*near_core(block), *in_hbm(whole))
+
+
+def hold_kernel(*refs):
+    ins, outs, sems = refs[: (len(refs) - 1) // 2], refs[(len(refs) - 1) // 2 : -1], refs[-1]
+    copies = [pltpu.make_async_copy(a, b, sems.at[i]) for i, (a, b) in enumerate(zip(ins, outs))]
+    for copy in copies:
+        copy.start()
+    for copy in copies:
+        copy.wait()
+
+
+def hold(*arrays):
+    return pl.pallas_call(
+        hold_kernel,
+        name="hold",
+        out_shape=[pltpu.VMEM(a.shape, a.dtype) for a in arrays],
+        in_specs=[ANY] * len(arrays),
+        out_specs=[VMEM] * len(arrays),
+        scratch_shapes=[pltpu.SemaphoreType.DMA((len(arrays),))],
+        compiler_params=limit(2),
+        cost_estimate=pl.CostEstimate(
+            flops=0, bytes_accessed=4 * sum(a.size for a in arrays), transcendentals=0
+        ),
+    )(*in_hbm(*arrays))
+
+
+def pair_body(expert_ids, gate_weights, hidden, hot_down, cold_down):
+    devices = lax.axis_size("expert")
+    near = [(i, i ^ 1) for i in range(devices)]
+    far = [(i, i ^ 2) for i in range(devices)]
+    tokens, _, _ = hidden.shape
+    cuts = [tokens * c // 16 for c in CUTS]
+    spans = list(zip(cuts[:-1], cuts[1:]))
+
+    def send(array, pairs):
+        return lax.ppermute(array, "expert", pairs)
+
+    held, moved, source = [], [], hidden
+    for i, (a, b) in enumerate(spans):
+        if i == 0:
+            rows, gates = take(source, a, b - a, (expert_ids.T, gate_weights.T))
+        else:
+            (rows,) = take(source, a, b - a)
+        held.append(rows)
+        moved.append(send(rows, far))
+    far_gates = send(gates, far)
+    partner = (send(cold_down, near), send(hot_down, near))
+    own = hold(cold_down, hot_down)
+    back = []
+    for i, (a, b) in enumerate(spans):
+        result = far_project(a, b - a, moved[i], far_gates, own, partner)
+        back.append(send(result, far))
+    out = own_project(devices, held, gates, own, partner)
+    for i, (a, _) in enumerate(spans):
+        out = put(a, back[i], out)
+    return out
+
+
 def solution(mesh):
-    return jax.shard_map(
-        body,
-        mesh=mesh,
-        in_specs=(
-            P(("dp", "expert"), None),
-            P(("dp", "expert"), None),
-            P(("dp", "expert"), None, None),
-            P(None, "expert"),
-            P(None, "expert"),
-        ),
-        out_specs=P(("dp", "expert"), None),
-        check_vma=False,
-    )
+    devices = mesh.shape["expert"]
+    specs = (
+        P(("dp", "expert"), None),
+        P(("dp", "expert"), None),
+        P(("dp", "expert"), None, None),
+        P(None, "expert"),
+        P(None, "expert"),
+    )
+
+    def spread(body):
+        return jax.shard_map(
+            body, mesh=mesh, in_specs=specs, out_specs=P(("dp", "expert"), None), check_vma=False
+        )
+
+    if devices != 4:
+        return spread(general_body)
+    return spread(pair_body)

time: 91.9 us -> 30.6 us (0.33)
  waiting for transfers between devices: 32.6 us -> 5.97 us
  blocking collectives: 24.4 us -> 0 us
  Pallas kernels: 0 us -> 14.5 us
  between operations: 13.5 us -> 0.12 us
  matrix products: 11.4 us -> 0 us
  starting transfers between devices: 3.64 us -> 9.88 us
  local copies, waits for them, and re-layouts: 3.85 us -> 0 us
  other arithmetic: 2.29 us -> 0 us
    all_to_all x1 -> x0, blocking collectives: 24.4 us -> none  [body(): lax.all_to_all(copies, 'expert', split_axis=0, concat_axis=0, tiled=True)]
    all_to_all x1 -> x0, waiting for transfers between devices: 20.6 us -> none  [body(): lax.all_to_all(outputs, 'expert', split_axis=0, concat_axis=0, tiled=True)]
    pallas_call x0 -> x11, Pallas kernels: none -> 14.5 us  [the longest x3 4.26 us: far_project(): pl.pallas_call(functools.partial(far_kernel, start), name='far_project',...]
    dot_general x4 -> x0, matrix products: 11.4 us -> none  [the longest x1 5.66 us: body(): jnp.dot(hot_rows, lax.all_gather(hot_down, 'expert', axis=1, tiled=True),...]
    all_gather x1 -> x0, waiting for transfers between devices: 11.3 us -> none  [body(): lax.all_gather(hot_down, 'expert', axis=1, tiled=True)]
    ppermute x0 -> x9, starting transfers between devices: none -> 9.88 us  [send(): return lax.ppermute(array, 'expert', pairs)]
    ppermute x0 -> x9, waiting for transfers between devices: none -> 5.97 us  [send(): return lax.ppermute(array, 'expert', pairs)]
    all_to_all x1 -> x0, starting transfers between devices: 3.64 us -> none  [body(): lax.all_to_all(outputs, 'expert', split_axis=0, concat_axis=0, tiled=True)]
  transfers between devices with their start and end apart: 2 -> 9, of which waited for: 2 -> 3; matrix products, arithmetic and copies ran while one was open for 13% -> 0% of each run, Pallas kernels for 0% -> 45%
where the time goes in v2:
time: 30.6 us; the launch traced here: 30.4 us
  Pallas kernels  14.5 us (47%)
  starting transfers between devices  9.88 us (32%)
  waiting for transfers between devices  5.97 us (20%)
    ppermute x9, starting transfers between devices, send(): return lax.ppermute(array, 'expert', pairs)  9.88 us
    ppermute x9, waiting for transfers between devices, send(): return lax.ppermute(array, 'expert', pairs)  5.97 us
    pallas_call x3, Pallas kernels, far_project(): pl.pallas_call(functools.partial(far_kernel, start), name='far_project',...  4.26 us
    pallas_call x1, Pallas kernels, own_project(): pl.pallas_call(own_kernel, name='own_project', out_shape=pltpu.HBM((token...  3.27 us
    pallas_call x3, Pallas kernels, take(): pl.pallas_call(functools.partial(first_take_kernel if choice else take_ke...  2.83 us
    pallas_call x1, Pallas kernels, hold(): pl.pallas_call(hold_kernel, name='hold', out_shape=[pltpu.VMEM(a.shape, a...  2.07 us
    pallas_call x3, Pallas kernels, put(): pl.pallas_call(functools.partial(put_kernel, start), name='put', out_shap...  2.04 us
  transfers between devices with their start and end apart: 9, of which 3 were waited for; matrix products, arithmetic and copies ran while one was open for 0% of the time, Pallas kernels for 45%

profile of v2, /device:TPU:0, one launch (start us, length us, event | category | flops | bytes accessed | tf_op | source)
XLA Modules:
  0.0 30.4 jit_solution(16826334983878484659)
XLA Ops:
  0.0 0.5 %collective-permute-start.3 = (bf16[1024,896]{1,0:T(8,128)(2,1)}, bf16[1024,896]{1,0:T(8,128)(2,1)S(1)}, u32[]{:S(2)}, u32[]{:S(2)}) collective-permute-start(bf16[1024,896]{1,0:T(8,128)(2,1)} %refs_1_.1), channel_id=1, source_target_pairs={{0,1},{1,0},{2,3},{3,2},{4,5},{5,4},{6,7},{7,6},{8,9},{9,8},{10,11... | collective-permute-start | bytes 5505032 | tf_op jit(solution)/shard_map/ppermute | solution.py:289
  0.5 0.0 collective-permute-start.2
  0.5 1.0 %take.5.refs_1_ = bf16[96,1024]{1,0:T(8,128)(2,1)S(1)} custom-call(bf16[128,2,1024]{2,1,0:T(2,128)(2,1)} %hidden_ref.5), custom_call_target="tpu_custom_call" | custom-call | bytes 393216 | tf_op jit(solution)/shard_map/take/pallas_call | solution.py:115
  1.5 3.0 %collective-permute-start.5 = (bf16[96,1024]{1,0:T(8,128)(2,1)S(1)}, bf16[96,1024]{1,0:T(8,128)(2,1)S(1)}, u32[]{:S(2)}, u32[]{:S(2)}) collective-permute-start(bf16[96,1024]{1,0:T(8,128)(2,1)S(1)} %take.5.refs_1_), channel_id=1, source_target_pairs={{0,2},{1,3},{2,0},{3,1},{4,6},{5,7},{6,4},{7,5},{8,10},{9,11},{10,... | collective-permute-start | bytes 589832 | tf_op jit(solution)/shard_map/ppermute | solution.py:289
  4.5 0.9 %take.4 = (bf16[80,1024]{1,0:T(8,128)(2,1)S(1)}, f32[4,128]{1,0:T(4,128)S(1)}) custom-call(bf16[128,2,1024]{2,1,0:T(2,128)(2,1)} %hidden_ref.5, s32[2,128]{1,0:T(2,128)} %bitcast.2, f32[2,128]{1,0:T(2,128)} %bitcast.3), custom_call_target="tpu_custom_call" | custom-call | bytes 327680 | tf_op jit(solution)/shard_map/take/pallas_call | solution.py:115
  5.5 0.1 collective-permute-start.7
  5.5 2.0 %collective-permute-start.1 = (f32[4,128]{1,0:T(4,128)S(1)}, f32[4,128]{1,0:T(4,128)S(1)}, u32[]{:S(2)}, u32[]{:S(2)}) collective-permute-start(f32[4,128]{1,0:T(4,128)S(1)} %get-tuple-element.9.refs_3_), channel_id=1, source_target_pairs={{0,2},{1,3},{2,0},{3,1},{4,6},{5,7},{6,4},{7,5},{8,10},{9,11},{10,... | collective-permute-start | bytes 6152 | tf_op jit(solution)/shard_map/ppermute | solution.py:289
  7.5 0.9 %take.3.refs_2_ = bf16[80,1024]{1,0:T(8,128)(2,1)S(1)} custom-call(bf16[128,2,1024]{2,1,0:T(2,128)(2,1)} %hidden_ref.5), custom_call_target="tpu_custom_call" | custom-call | bytes 327680 | tf_op jit(solution)/shard_map/take/pallas_call | solution.py:115
  8.5 4.6 %collective-permute-done.1.gates_ref = f32[4,128]{1,0:T(4,128)S(1)} collective-permute-done((f32[4,128]{1,0:T(4,128)S(1)}, f32[4,128]{1,0:T(4,128)S(1)}, u32[]{:S(2)}, u32[]{:S(2)}) %collective-permute-start.1) | collective-permute-done | bytes 2080 | tf_op jit(solution)/shard_map/ppermute | solution.py:289
  13.1 1.7 %collective-permute-start = (bf16[80,1024]{1,0:T(8,128)(2,1)S(1)}, bf16[80,1024]{1,0:T(8,128)(2,1)S(1)}, u32[]{:S(2)}, u32[]{:S(2)}) collective-permute-start(bf16[80,1024]{1,0:T(8,128)(2,1)S(1)} %take.3.refs_2_), channel_id=1, source_target_pairs={{0,2},{1,3},{2,0},{3,1},{4,6},{5,7},{6,4},{7,5},{8,10},{9,11},{10,... | collective-permute-start | bytes 491528 | tf_op jit(solution)/shard_map/ppermute | solution.py:289
  14.9 2.1 %hold.1 = (bf16[1024,896]{1,0:T(8,128)(2,1)S(1)}, bf16[1024,896]{1,0:T(8,128)(2,1)S(1)}) custom-call(bf16[1024,896]{1,0:T(8,128)(2,1)} %refs_0_.1, bf16[1024,896]{1,0:T(8,128)(2,1)} %refs_1_.1), custom_call_target="tpu_custom_call" | custom-call | bytes 7340032 | tf_op jit(solution)/shard_map/hold/pallas_call | solution.py:266
  16.9 0.0 collective-permute-done.5.rows_ref
  17.0 1.4 %far_project.4 = bf16[48,1792]{1,0:T(8,128)(2,1)S(1)} custom-call(bf16[96,1024]{1,0:T(8,128)(2,1)S(1)} %collective-permute-done.5.rows_ref, f32[4,128]{1,0:T(4,128)S(1)} %collective-permute-done.1.gates_ref, bf16[1024,896]{1,0:T(8,128)(2,1)S(1)} %get-tuple-element.10.c0.refs_4_, bf16[1024,896]{1,0:T(8,128)(2,1)S(1)} %get-tuple-element.11.h0.refs_5_, ...), custom_call_target="tpu_custom_call" | custom-call | flops 352321536 | bytes 688128 | tf_op jit(solution)/shard_map/far_project/pallas_call | solution.py:172
  18.4 0.4 %collective-permute-start.6 = (bf16[48,1792]{1,0:T(8,128)(2,1)S(1)}, bf16[48,1792]{1,0:T(8,128)(2,1)S(1)}, u32[]{:S(2)}, u32[]{:S(2)}) collective-permute-start(bf16[48,1792]{1,0:T(8,128)(2,1)S(1)} %far_project.4), channel_id=1, source_target_pairs={{0,2},{1,3},{2,0},{3,1},{4,6},{5,7},{6,4},{7,5},{8,10},{9,11},{10,... | collective-permute-start | bytes 516104 | tf_op jit(solution)/shard_map/ppermute | solution.py:289
  18.8 1.4 %far_project.5 = bf16[40,1792]{1,0:T(8,128)(2,1)S(1)} custom-call(bf16[80,1024]{1,0:T(8,128)(2,1)S(1)} %collective-permute-done.7.rows_ref, f32[4,128]{1,0:T(4,128)S(1)} %collective-permute-done.1.gates_ref, bf16[1024,896]{1,0:T(8,128)(2,1)S(1)} %get-tuple-element.10.c0.refs_4_, bf16[1024,896]{1,0:T(8,128)(2,1)S(1)} %get-tuple-element.11.h0.refs_5_, ...), custom_call_target="tpu_custom_call" | custom-call | flops 293601280 | bytes 573440 | tf_op jit(solution)/shard_map/far_project/pallas_call | solution.py:172
  20.2 1.8 %collective-permute-start.8 = (bf16[40,1792]{1,0:T(8,128)(2,1)S(1)}, bf16[40,1792]{1,0:T(8,128)(2,1)S(1)}, u32[]{:S(2)}, u32[]{:S(2)}) collective-permute-start(bf16[40,1792]{1,0:T(8,128)(2,1)S(1)} %far_project.5), channel_id=1, source_target_pairs={{0,2},{1,3},{2,0},{3,1},{4,6},{5,7},{6,4},{7,5},{8,10},{9,11},{10,... | collective-permute-start | bytes 430088 | tf_op jit(solution)/shard_map/ppermute | solution.py:289
  22.0 1.4 %far_project.3 = bf16[40,1792]{1,0:T(8,128)(2,1)S(1)} custom-call(bf16[80,1024]{1,0:T(8,128)(2,1)S(1)} %collective-permute-done.rows_ref, f32[4,128]{1,0:T(4,128)S(1)} %collective-permute-done.1.gates_ref, bf16[1024,896]{1,0:T(8,128)(2,1)S(1)} %get-tuple-element.10.c0.refs_4_, bf16[1024,896]{1,0:T(8,128)(2,1)S(1)} %get-tuple-element.11.h0.refs_5_, ...), custom_call_target="tpu_custom_call" | custom-call | flops 293601280 | bytes 573440 | tf_op jit(solution)/shard_map/far_project/pallas_call | solution.py:172
  23.4 0.3 %collective-permute-start.4 = (bf16[40,1792]{1,0:T(8,128)(2,1)S(1)}, bf16[40,1792]{1,0:T(8,128)(2,1)S(1)}, u32[]{:S(2)}, u32[]{:S(2)}) collective-permute-start(bf16[40,1792]{1,0:T(8,128)(2,1)S(1)} %far_project.3), channel_id=1, source_target_pairs={{0,2},{1,3},{2,0},{3,1},{4,6},{5,7},{6,4},{7,5},{8,10},{9,11},{10,... | collective-permute-start | bytes 430088 | tf_op jit(solution)/shard_map/ppermute | solution.py:289
  23.8 3.3 %own_project.1.whole_ref = bf16[128,3584]{1,0:T(8,128)(2,1)} custom-call(bf16[80,1024]{1,0:T(8,128)(2,1)S(1)} %get-tuple-element.12.refs_0_, bf16[96,1024]{1,0:T(8,128)(2,1)S(1)} %take.5.refs_1_, bf16[80,1024]{1,0:T(8,128)(2,1)S(1)} %take.3.refs_2_, f32[4,128]{1,0:T(4,128)S(1)} %get-tuple-element.9.refs_3_, ...), custom_call_target="tpu_custom_call" | custom-call | flops 880803840 | bytes 1720320 | tf_op jit(solution)/shard_map/own_project/pallas_call | solution.py:211
  27.1 1.2 %collective-permute-done.8.block_ref = bf16[40,1792]{1,0:T(8,128)(2,1)S(1)} collective-permute-done((bf16[40,1792]{1,0:T(8,128)(2,1)S(1)}, bf16[40,1792]{1,0:T(8,128)(2,1)S(1)}, u32[]{:S(2)}, u32[]{:S(2)}) %collective-permute-start.8) | collective-permute-done | bytes 143392 | tf_op jit(solution)/shard_map/ppermute | solution.py:289
  28.2 0.7 %put.3.whole_ref = bf16[128,3584]{1,0:T(8,128)(2,1)} custom-call(bf16[40,1792]{1,0:T(8,128)(2,1)S(1)} %collective-permute-done.8.block_ref, bf16[128,3584]{1,0:T(8,128)(2,1)} %own_project.1.whole_ref), custom_call_target="tpu_custom_call", output_to_operand_aliasing={{}: (1, {})} | custom-call | bytes 286720 | tf_op jit(solution)/shard_map/put/pallas_call | solution.py:243
  28.9 0.7 %put.4.whole_ref = bf16[128,3584]{1,0:T(8,128)(2,1)} custom-call(bf16[48,1792]{1,0:T(8,128)(2,1)S(1)} %collective-permute-done.6.block_ref, bf16[128,3584]{1,0:T(8,128)(2,1)} %put.3.whole_ref), custom_call_target="tpu_custom_call", output_to_operand_aliasing={{}: (1, {})} | custom-call | bytes 344064 | tf_op jit(solution)/shard_map/put/pallas_call | solution.py:243
  29.6 0.1 collective-permute-done.4.block_ref
  29.8 0.7 %put.5 = bf16[128,3584]{1,0:T(8,128)(2,1)} custom-call(bf16[40,1792]{1,0:T(8,128)(2,1)S(1)} %collective-permute-done.4.block_ref, bf16[128,3584]{1,0:T(8,128)(2,1)} %put.4.whole_ref), custom_call_target="tpu_custom_call", output_to_operand_aliasing={{}: (1, {})} | custom-call | bytes 286720 | tf_op jit(solution)/shard_map/put/pallas_call | solution.py:243
  (5 shorter events, 0.0 us)
Async XLA Ops:
  0.0 17.0 %collective-permute-start.3 = (bf16[1024,896]{1,0:T(8,128)(2,1)}, bf16[1024,896]{1,0:T(8,128)(2,1)S(1)}, u32[]{:S(2)}, u32[]{:S(2)}) collective-permute-start(bf16[1024,896]{1,0:T(8,128)(2,1)} %refs_1_.1), channel_id=1, source_target_pairs={{0,1},{1,0},{2,3},{3,2},{4,5},{5,4},{6,7},{7,6},{8,9},{9,8},{10,11... | collective-permute-start | bytes 5505032 | tf_op jit(solution)/shard_map/ppermute | solution.py:289
  0.5 16.5 %collective-permute-start.2 = (bf16[1024,896]{1,0:T(8,128)(2,1)}, bf16[1024,896]{1,0:T(8,128)(2,1)S(1)}, u32[]{:S(2)}, u32[]{:S(2)}) collective-permute-start(bf16[1024,896]{1,0:T(8,128)(2,1)} %refs_0_.1), channel_id=1, source_target_pairs={{0,1},{1,0},{2,3},{3,2},{4,5},{5,4},{6,7},{7,6},{8,9},{9,8},{10,11... | collective-permute-start | bytes 5505032 | tf_op jit(solution)/shard_map/ppermute | solution.py:289
  1.5 15.5 %collective-permute-start.5 = (bf16[96,1024]{1,0:T(8,128)(2,1)S(1)}, bf16[96,1024]{1,0:T(8,128)(2,1)S(1)}, u32[]{:S(2)}, u32[]{:S(2)}) collective-permute-start(bf16[96,1024]{1,0:T(8,128)(2,1)S(1)} %take.5.refs_1_), channel_id=1, source_target_pairs={{0,2},{1,3},{2,0},{3,1},{4,6},{5,7},{6,4},{7,5},{8,10},{9,11},{10,... | collective-permute-start | bytes 589832 | tf_op jit(solution)/shard_map/ppermute | solution.py:289
  5.5 13.3 %collective-permute-start.7 = (bf16[80,1024]{1,0:T(8,128)(2,1)S(1)}, bf16[80,1024]{1,0:T(8,128)(2,1)S(1)}, u32[]{:S(2)}, u32[]{:S(2)}) collective-permute-start(bf16[80,1024]{1,0:T(8,128)(2,1)S(1)} %get-tuple-element.12.refs_0_), channel_id=1, source_target_pairs={{0,2},{1,3},{2,0},{3,1},{4,6},{5,7},{6,4},{7,5},{8,10},{9,11},{10,... | collective-permute-start | bytes 491528 | tf_op jit(solution)/shard_map/ppermute | solution.py:289
  5.5 7.6 %collective-permute-start.1 = (f32[4,128]{1,0:T(4,128)S(1)}, f32[4,128]{1,0:T(4,128)S(1)}, u32[]{:S(2)}, u32[]{:S(2)}) collective-permute-start(f32[4,128]{1,0:T(4,128)S(1)} %get-tuple-element.9.refs_3_), channel_id=1, source_target_pairs={{0,2},{1,3},{2,0},{3,1},{4,6},{5,7},{6,4},{7,5},{8,10},{9,11},{10,... | collective-permute-start | bytes 6152 | tf_op jit(solution)/shard_map/ppermute | solution.py:289
  13.1 8.9 %collective-permute-start = (bf16[80,1024]{1,0:T(8,128)(2,1)S(1)}, bf16[80,1024]{1,0:T(8,128)(2,1)S(1)}, u32[]{:S(2)}, u32[]{:S(2)}) collective-permute-start(bf16[80,1024]{1,0:T(8,128)(2,1)S(1)} %take.3.refs_2_), channel_id=1, source_target_pairs={{0,2},{1,3},{2,0},{3,1},{4,6},{5,7},{6,4},{7,5},{8,10},{9,11},{10,... | collective-permute-start | bytes 491528 | tf_op jit(solution)/shard_map/ppermute | solution.py:289
  18.4 10.5 %collective-permute-start.6 = (bf16[48,1792]{1,0:T(8,128)(2,1)S(1)}, bf16[48,1792]{1,0:T(8,128)(2,1)S(1)}, u32[]{:S(2)}, u32[]{:S(2)}) collective-permute-start(bf16[48,1792]{1,0:T(8,128)(2,1)S(1)} %far_project.4), channel_id=1, source_target_pairs={{0,2},{1,3},{2,0},{3,1},{4,6},{5,7},{6,4},{7,5},{8,10},{9,11},{10,... | collective-permute-start | bytes 516104 | tf_op jit(solution)/shard_map/ppermute | solution.py:289
  20.2 8.1 %collective-permute-start.8 = (bf16[40,1792]{1,0:T(8,128)(2,1)S(1)}, bf16[40,1792]{1,0:T(8,128)(2,1)S(1)}, u32[]{:S(2)}, u32[]{:S(2)}) collective-permute-start(bf16[40,1792]{1,0:T(8,128)(2,1)S(1)} %far_project.5), channel_id=1, source_target_pairs={{0,2},{1,3},{2,0},{3,1},{4,6},{5,7},{6,4},{7,5},{8,10},{9,11},{10,... | collective-permute-start | bytes 430088 | tf_op jit(solution)/shard_map/ppermute | solution.py:289
  23.4 6.3 %collective-permute-start.4 = (bf16[40,1792]{1,0:T(8,128)(2,1)S(1)}, bf16[40,1792]{1,0:T(8,128)(2,1)S(1)}, u32[]{:S(2)}, u32[]{:S(2)}) collective-permute-start(bf16[40,1792]{1,0:T(8,128)(2,1)S(1)} %far_project.3), channel_id=1, source_target_pairs={{0,2},{1,3},{2,0},{3,1},{4,6},{5,7},{6,4},{7,5},{8,10},{9,11},{10,... | collective-permute-start | bytes 430088 | tf_op jit(solution)/shard_map/ppermute | solution.py:289

commit v3 on v2

--- a/solution.py
+++ b/solution.py
@@ -10,6 +10,7 @@
 VMEM = pl.BlockSpec(memory_space=pltpu.VMEM)
 ANY = pl.BlockSpec(memory_space=pl.ANY)
 SLAB = 128
+PARTS = 5
 CUTS = (0, 5, 11, 16)
 
 
@@ -79,36 +80,47 @@
     return pltpu.CompilerParams(vmem_limit_bytes=mib << 20)
 
 
-def rows_of(hidden_ref, start, rows_ref, sem):
+def rows_of(hidden_ref, start, rows_ref, sems):
     flat = hidden_ref.reshape(hidden_ref.shape[0] * hidden_ref.shape[1], hidden_ref.shape[2])
-    return pltpu.make_async_copy(flat.at[pl.ds(start, rows_ref.shape[0])], rows_ref, sem)
+    total = rows_ref.shape[0]
+    parts = max(p for p in range(1, PARTS + 1) if total % (8 * p) == 0)
+    count = total // parts
+    return [
+        pltpu.make_async_copy(
+            flat.at[pl.ds(start + i * count, count)], rows_ref.at[pl.ds(i * count, count)], sems.at[i]
+        )
+        for i in range(parts)
+    ]
 
 
 def take_kernel(start, hidden_ref, rows_ref, sems):
-    copy = rows_of(hidden_ref, start, rows_ref, sems.at[0])
-    copy.start()
-    copy.wait()
+    copies = rows_of(hidden_ref, start, rows_ref, sems)
+    for copy in copies:
+        copy.start()
+    for copy in copies:
+        copy.wait()
 
 
 def first_take_kernel(start, hidden_ref, ids_ref, weights_ref, rows_ref, gates_ref, ids, weights, sems):
-    copies = [
-        rows_of(hidden_ref, start, rows_ref, sems.at[0]),
-        pltpu.make_async_copy(ids_ref, ids, sems.at[1]),
-        pltpu.make_async_copy(weights_ref, weights, sems.at[2]),
+    large = rows_of(hidden_ref, start, rows_ref, sems)
+    small = [
+        pltpu.make_async_copy(ids_ref, ids, sems.at[PARTS]),
+        pltpu.make_async_copy(weights_ref, weights, sems.at[PARTS + 1]),
     ]
-    for copy in copies:
+    for copy in large + small:
         copy.start()
-    for copy in copies[1:]:
+    for copy in small:
         copy.wait()
     for e in range(2):
         gates_ref[2 * e : 2 * e + 2, :] = jnp.where(ids[...] == e, weights[...], 0.0)
-    copies[0].wait()
+    for copy in large:
+        copy.wait()
 
 
 def take(hidden, start, tokens, choice=()):
     _, choices, depth = hidden.shape
     shapes = [pltpu.VMEM((tokens * choices, depth), hidden.dtype)]
-    scratch = [pltpu.SemaphoreType.DMA((3,))]
+    scratch = [pltpu.SemaphoreType.DMA((PARTS + 2,))]
     if choice:
         shapes.append(pltpu.VMEM((2 * choices, hidden.shape[0]), choice[1].dtype))
         scratch = [pltpu.VMEM(c.shape, c.dtype) for c in choice] + scratch
@@ -290,7 +302,7 @@
 
     held, moved, source = [], [], hidden
     for i, (a, b) in enumerate(spans):
-        if i == 0:
+        if i == 1:
             rows, gates = take(source, a, b - a, (expert_ids.T, gate_weights.T))
         else:
             (rows,) = take(source, a, b - a)

time: 30.6 us -> 30.7 us (level)
  no operation moved by 1% of the time
where the time goes in v3:
time: 30.7 us; the launch traced here: 30.4 us
  Pallas kernels  14.3 us (47%)
  starting transfers between devices  9.88 us (32%)
  waiting for transfers between devices  6.08 us (20%)
    ppermute x9, starting transfers between devices, send(): return lax.ppermute(array, 'expert', pairs)  9.88 us
    ppermute x9, waiting for transfers between devices, send(): return lax.ppermute(array, 'expert', pairs)  6.08 us
    pallas_call x3, Pallas kernels, far_project(): pl.pallas_call(functools.partial(far_kernel, start), name='far_project',...  4.26 us
    pallas_call x1, Pallas kernels, own_project(): pl.pallas_call(own_kernel, name='own_project', out_shape=pltpu.HBM((token...  3.27 us
    pallas_call x3, Pallas kernels, take(): pl.pallas_call(functools.partial(first_take_kernel if choice else take_ke...  2.69 us
    pallas_call x1, Pallas kernels, hold(): pl.pallas_call(hold_kernel, name='hold', out_shape=[pltpu.VMEM(a.shape, a...  2.07 us
    pallas_call x3, Pallas kernels, put(): pl.pallas_call(functools.partial(put_kernel, start), name='put', out_shap...  2.04 us
  transfers between devices with their start and end apart: 9, of which 3 were waited for; matrix products, arithmetic and copies ran while one was open for 0% of the time, Pallas kernels for 45%

profile of v3, /device:TPU:0, one launch (start us, length us, event | category | flops | bytes accessed | tf_op | source)
XLA Modules:
  0.0 30.4 jit_solution(2137464003944587382)
XLA Ops:
  0.0 0.5 %collective-permute-start.3 = (bf16[1024,896]{1,0:T(8,128)(2,1)}, bf16[1024,896]{1,0:T(8,128)(2,1)S(1)}, u32[]{:S(2)}, u32[]{:S(2)}) collective-permute-start(bf16[1024,896]{1,0:T(8,128)(2,1)} %refs_1_.1), channel_id=1, source_target_pairs={{0,1},{1,0},{2,3},{3,2},{4,5},{5,4},{6,7},{7,6},{8,9},{9,8},{10,11... | collective-permute-start | bytes 5505032 | tf_op jit(solution)/shard_map/ppermute | solution.py:301
  0.5 0.0 collective-permute-start.2
  0.5 0.9 %take.4 = (bf16[96,1024]{1,0:T(8,128)(2,1)S(1)}, f32[4,128]{1,0:T(4,128)S(1)}) custom-call(bf16[128,2,1024]{2,1,0:T(2,128)(2,1)} %hidden_ref.5, s32[2,128]{1,0:T(2,128)} %bitcast.2, f32[2,128]{1,0:T(2,128)} %bitcast.3), custom_call_target="tpu_custom_call" | custom-call | bytes 393216 | tf_op jit(solution)/shard_map/take/pallas_call | solution.py:127
  1.4 3.0 %collective-permute-start.5 = (bf16[96,1024]{1,0:T(8,128)(2,1)S(1)}, bf16[96,1024]{1,0:T(8,128)(2,1)S(1)}, u32[]{:S(2)}, u32[]{:S(2)}) collective-permute-start(bf16[96,1024]{1,0:T(8,128)(2,1)S(1)} %get-tuple-element.12.refs_1_), channel_id=1, source_target_pairs={{0,2},{1,3},{2,0},{3,1},{4,6},{5,7},{6,4},{7,5},{8,10},{9,11},{10,... | collective-permute-start | bytes 589832 | tf_op jit(solution)/shard_map/ppermute | solution.py:301
  4.5 0.9 %take.5.refs_0_ = bf16[80,1024]{1,0:T(8,128)(2,1)S(1)} custom-call(bf16[128,2,1024]{2,1,0:T(2,128)(2,1)} %hidden_ref.5), custom_call_target="tpu_custom_call" | custom-call | bytes 327680 | tf_op jit(solution)/shard_map/take/pallas_call | solution.py:127
  5.4 0.1 collective-permute-start.7
  5.5 2.0 %collective-permute-start.1 = (f32[4,128]{1,0:T(4,128)S(1)}, f32[4,128]{1,0:T(4,128)S(1)}, u32[]{:S(2)}, u32[]{:S(2)}) collective-permute-start(f32[4,128]{1,0:T(4,128)S(1)} %get-tuple-element.9.refs_3_), channel_id=1, source_target_pairs={{0,2},{1,3},{2,0},{3,1},{4,6},{5,7},{6,4},{7,5},{8,10},{9,11},{10,... | collective-permute-start | bytes 6152 | tf_op jit(solution)/shard_map/ppermute | solution.py:301
  7.5 0.9 %take.3.refs_2_ = bf16[80,1024]{1,0:T(8,128)(2,1)S(1)} custom-call(bf16[128,2,1024]{2,1,0:T(2,128)(2,1)} %hidden_ref.5), custom_call_target="tpu_custom_call" | custom-call | bytes 327680 | tf_op jit(solution)/shard_map/take/pallas_call | solution.py:127
  8.4 4.8 %collective-permute-done.1.gates_ref = f32[4,128]{1,0:T(4,128)S(1)} collective-permute-done((f32[4,128]{1,0:T(4,128)S(1)}, f32[4,128]{1,0:T(4,128)S(1)}, u32[]{:S(2)}, u32[]{:S(2)}) %collective-permute-start.1) | collective-permute-done | bytes 2080 | tf_op jit(solution)/shard_map/ppermute | solution.py:301
  13.1 1.7 %collective-permute-start = (bf16[80,1024]{1,0:T(8,128)(2,1)S(1)}, bf16[80,1024]{1,0:T(8,128)(2,1)S(1)}, u32[]{:S(2)}, u32[]{:S(2)}) collective-permute-start(bf16[80,1024]{1,0:T(8,128)(2,1)S(1)} %take.3.refs_2_), channel_id=1, source_target_pairs={{0,2},{1,3},{2,0},{3,1},{4,6},{5,7},{6,4},{7,5},{8,10},{9,11},{10,... | collective-permute-start | bytes 491528 | tf_op jit(solution)/shard_map/ppermute | solution.py:301
  14.8 2.1 %hold.1 = (bf16[1024,896]{1,0:T(8,128)(2,1)S(1)}, bf16[1024,896]{1,0:T(8,128)(2,1)S(1)}) custom-call(bf16[1024,896]{1,0:T(8,128)(2,1)} %refs_0_.1, bf16[1024,896]{1,0:T(8,128)(2,1)} %refs_1_.1), custom_call_target="tpu_custom_call" | custom-call | bytes 7340032 | tf_op jit(solution)/shard_map/hold/pallas_call | solution.py:278
  16.9 0.0 collective-permute-done.5.rows_ref
  17.0 1.4 %far_project.4 = bf16[48,1792]{1,0:T(8,128)(2,1)S(1)} custom-call(bf16[96,1024]{1,0:T(8,128)(2,1)S(1)} %collective-permute-done.5.rows_ref, f32[4,128]{1,0:T(4,128)S(1)} %collective-permute-done.1.gates_ref, bf16[1024,896]{1,0:T(8,128)(2,1)S(1)} %get-tuple-element.10.c0.refs_4_, bf16[1024,896]{1,0:T(8,128)(2,1)S(1)} %get-tuple-element.11.h0.refs_5_, ...), custom_call_target="tpu_custom_call" | custom-call | flops 352321536 | bytes 688128 | tf_op jit(solution)/shard_map/far_project/pallas_call | solution.py:184
  18.4 0.4 %collective-permute-start.6 = (bf16[48,1792]{1,0:T(8,128)(2,1)S(1)}, bf16[48,1792]{1,0:T(8,128)(2,1)S(1)}, u32[]{:S(2)}, u32[]{:S(2)}) collective-permute-start(bf16[48,1792]{1,0:T(8,128)(2,1)S(1)} %far_project.4), channel_id=1, source_target_pairs={{0,2},{1,3},{2,0},{3,1},{4,6},{5,7},{6,4},{7,5},{8,10},{9,11},{10,... | collective-permute-start | bytes 516104 | tf_op jit(solution)/shard_map/ppermute | solution.py:301
  18.7 1.4 %far_project.5 = bf16[40,1792]{1,0:T(8,128)(2,1)S(1)} custom-call(bf16[80,1024]{1,0:T(8,128)(2,1)S(1)} %collective-permute-done.7.rows_ref, f32[4,128]{1,0:T(4,128)S(1)} %collective-permute-done.1.gates_ref, bf16[1024,896]{1,0:T(8,128)(2,1)S(1)} %get-tuple-element.10.c0.refs_4_, bf16[1024,896]{1,0:T(8,128)(2,1)S(1)} %get-tuple-element.11.h0.refs_5_, ...), custom_call_target="tpu_custom_call" | custom-call | flops 293601280 | bytes 573440 | tf_op jit(solution)/shard_map/far_project/pallas_call | solution.py:184
  20.2 1.8 %collective-permute-start.8 = (bf16[40,1792]{1,0:T(8,128)(2,1)S(1)}, bf16[40,1792]{1,0:T(8,128)(2,1)S(1)}, u32[]{:S(2)}, u32[]{:S(2)}) collective-permute-start(bf16[40,1792]{1,0:T(8,128)(2,1)S(1)} %far_project.5), channel_id=1, source_target_pairs={{0,2},{1,3},{2,0},{3,1},{4,6},{5,7},{6,4},{7,5},{8,10},{9,11},{10,... | collective-permute-start | bytes 430088 | tf_op jit(solution)/shard_map/ppermute | solution.py:301
  22.0 1.4 %far_project.3 = bf16[40,1792]{1,0:T(8,128)(2,1)S(1)} custom-call(bf16[80,1024]{1,0:T(8,128)(2,1)S(1)} %collective-permute-done.rows_ref, f32[4,128]{1,0:T(4,128)S(1)} %collective-permute-done.1.gates_ref, bf16[1024,896]{1,0:T(8,128)(2,1)S(1)} %get-tuple-element.10.c0.refs_4_, bf16[1024,896]{1,0:T(8,128)(2,1)S(1)} %get-tuple-element.11.h0.refs_5_, ...), custom_call_target="tpu_custom_call" | custom-call | flops 293601280 | bytes 573440 | tf_op jit(solution)/shard_map/far_project/pallas_call | solution.py:184
  23.4 0.3 %collective-permute-start.4 = (bf16[40,1792]{1,0:T(8,128)(2,1)S(1)}, bf16[40,1792]{1,0:T(8,128)(2,1)S(1)}, u32[]{:S(2)}, u32[]{:S(2)}) collective-permute-start(bf16[40,1792]{1,0:T(8,128)(2,1)S(1)} %far_project.3), channel_id=1, source_target_pairs={{0,2},{1,3},{2,0},{3,1},{4,6},{5,7},{6,4},{7,5},{8,10},{9,11},{10,... | collective-permute-start | bytes 430088 | tf_op jit(solution)/shard_map/ppermute | solution.py:301
  23.8 3.3 %own_project.1.whole_ref = bf16[128,3584]{1,0:T(8,128)(2,1)} custom-call(bf16[80,1024]{1,0:T(8,128)(2,1)S(1)} %take.5.refs_0_, bf16[96,1024]{1,0:T(8,128)(2,1)S(1)} %get-tuple-element.12.refs_1_, bf16[80,1024]{1,0:T(8,128)(2,1)S(1)} %take.3.refs_2_, f32[4,128]{1,0:T(4,128)S(1)} %get-tuple-element.9.refs_3_, ...), custom_call_target="tpu_custom_call" | custom-call | flops 880803840 | bytes 1720320 | tf_op jit(solution)/shard_map/own_project/pallas_call | solution.py:223
  27.0 1.2 %collective-permute-done.8.block_ref = bf16[40,1792]{1,0:T(8,128)(2,1)S(1)} collective-permute-done((bf16[40,1792]{1,0:T(8,128)(2,1)S(1)}, bf16[40,1792]{1,0:T(8,128)(2,1)S(1)}, u32[]{:S(2)}, u32[]{:S(2)}) %collective-permute-start.8) | collective-permute-done | bytes 143392 | tf_op jit(solution)/shard_map/ppermute | solution.py:301
  28.2 0.7 %put.3.whole_ref = bf16[128,3584]{1,0:T(8,128)(2,1)} custom-call(bf16[40,1792]{1,0:T(8,128)(2,1)S(1)} %collective-permute-done.8.block_ref, bf16[128,3584]{1,0:T(8,128)(2,1)} %own_project.1.whole_ref), custom_call_target="tpu_custom_call", output_to_operand_aliasing={{}: (1, {})} | custom-call | bytes 286720 | tf_op jit(solution)/shard_map/put/pallas_call | solution.py:255
  28.9 0.7 %put.4.whole_ref = bf16[128,3584]{1,0:T(8,128)(2,1)} custom-call(bf16[48,1792]{1,0:T(8,128)(2,1)S(1)} %collective-permute-done.6.block_ref, bf16[128,3584]{1,0:T(8,128)(2,1)} %put.3.whole_ref), custom_call_target="tpu_custom_call", output_to_operand_aliasing={{}: (1, {})} | custom-call | bytes 344064 | tf_op jit(solution)/shard_map/put/pallas_call | solution.py:255
  29.6 0.1 collective-permute-done.4.block_ref
  29.7 0.7 %put.5 = bf16[128,3584]{1,0:T(8,128)(2,1)} custom-call(bf16[40,1792]{1,0:T(8,128)(2,1)S(1)} %collective-permute-done.4.block_ref, bf16[128,3584]{1,0:T(8,128)(2,1)} %put.4.whole_ref), custom_call_target="tpu_custom_call", output_to_operand_aliasing={{}: (1, {})} | custom-call | bytes 286720 | tf_op jit(solution)/shard_map/put/pallas_call | solution.py:255
  (5 shorter events, 0.0 us)
Async XLA Ops:
  0.0 16.9 %collective-permute-start.3 = (bf16[1024,896]{1,0:T(8,128)(2,1)}, bf16[1024,896]{1,0:T(8,128)(2,1)S(1)}, u32[]{:S(2)}, u32[]{:S(2)}) collective-permute-start(bf16[1024,896]{1,0:T(8,128)(2,1)} %refs_1_.1), channel_id=1, source_target_pairs={{0,1},{1,0},{2,3},{3,2},{4,5},{5,4},{6,7},{7,6},{8,9},{9,8},{10,11... | collective-permute-start | bytes 5505032 | tf_op jit(solution)/shard_map/ppermute | solution.py:301
  0.5 16.5 %collective-permute-start.2 = (bf16[1024,896]{1,0:T(8,128)(2,1)}, bf16[1024,896]{1,0:T(8,128)(2,1)S(1)}, u32[]{:S(2)}, u32[]{:S(2)}) collective-permute-start(bf16[1024,896]{1,0:T(8,128)(2,1)} %refs_0_.1), channel_id=1, source_target_pairs={{0,1},{1,0},{2,3},{3,2},{4,5},{5,4},{6,7},{7,6},{8,9},{9,8},{10,11... | collective-permute-start | bytes 5505032 | tf_op jit(solution)/shard_map/ppermute | solution.py:301
  1.4 15.5 %collective-permute-start.5 = (bf16[96,1024]{1,0:T(8,128)(2,1)S(1)}, bf16[96,1024]{1,0:T(8,128)(2,1)S(1)}, u32[]{:S(2)}, u32[]{:S(2)}) collective-permute-start(bf16[96,1024]{1,0:T(8,128)(2,1)S(1)} %get-tuple-element.12.refs_1_), channel_id=1, source_target_pairs={{0,2},{1,3},{2,0},{3,1},{4,6},{5,7},{6,4},{7,5},{8,10},{9,11},{10,... | collective-permute-start | bytes 589832 | tf_op jit(solution)/shard_map/ppermute | solution.py:301
  5.4 13.4 %collective-permute-start.7 = (bf16[80,1024]{1,0:T(8,128)(2,1)S(1)}, bf16[80,1024]{1,0:T(8,128)(2,1)S(1)}, u32[]{:S(2)}, u32[]{:S(2)}) collective-permute-start(bf16[80,1024]{1,0:T(8,128)(2,1)S(1)} %take.5.refs_0_), channel_id=1, source_target_pairs={{0,2},{1,3},{2,0},{3,1},{4,6},{5,7},{6,4},{7,5},{8,10},{9,11},{10,... | collective-permute-start | bytes 491528 | tf_op jit(solution)/shard_map/ppermute | solution.py:301
  5.5 7.6 %collective-permute-start.1 = (f32[4,128]{1,0:T(4,128)S(1)}, f32[4,128]{1,0:T(4,128)S(1)}, u32[]{:S(2)}, u32[]{:S(2)}) collective-permute-start(f32[4,128]{1,0:T(4,128)S(1)} %get-tuple-element.9.refs_3_), channel_id=1, source_target_pairs={{0,2},{1,3},{2,0},{3,1},{4,6},{5,7},{6,4},{7,5},{8,10},{9,11},{10,... | collective-permute-start | bytes 6152 | tf_op jit(solution)/shard_map/ppermute | solution.py:301
  13.1 8.9 %collective-permute-start = (bf16[80,1024]{1,0:T(8,128)(2,1)S(1)}, bf16[80,1024]{1,0:T(8,128)(2,1)S(1)}, u32[]{:S(2)}, u32[]{:S(2)}) collective-permute-start(bf16[80,1024]{1,0:T(8,128)(2,1)S(1)} %take.3.refs_2_), channel_id=1, source_target_pairs={{0,2},{1,3},{2,0},{3,1},{4,6},{5,7},{6,4},{7,5},{8,10},{9,11},{10,... | collective-permute-start | bytes 491528 | tf_op jit(solution)/shard_map/ppermute | solution.py:301
  18.4 10.5 %collective-permute-start.6 = (bf16[48,1792]{1,0:T(8,128)(2,1)S(1)}, bf16[48,1792]{1,0:T(8,128)(2,1)S(1)}, u32[]{:S(2)}, u32[]{:S(2)}) collective-permute-start(bf16[48,1792]{1,0:T(8,128)(2,1)S(1)} %far_project.4), channel_id=1, source_target_pairs={{0,2},{1,3},{2,0},{3,1},{4,6},{5,7},{6,4},{7,5},{8,10},{9,11},{10,... | collective-permute-start | bytes 516104 | tf_op jit(solution)/shard_map/ppermute | solution.py:301
  20.2 8.0 %collective-permute-start.8 = (bf16[40,1792]{1,0:T(8,128)(2,1)S(1)}, bf16[40,1792]{1,0:T(8,128)(2,1)S(1)}, u32[]{:S(2)}, u32[]{:S(2)}) collective-permute-start(bf16[40,1792]{1,0:T(8,128)(2,1)S(1)} %far_project.5), channel_id=1, source_target_pairs={{0,2},{1,3},{2,0},{3,1},{4,6},{5,7},{6,4},{7,5},{8,10},{9,11},{10,... | collective-permute-start | bytes 430088 | tf_op jit(solution)/shard_map/ppermute | solution.py:301
  23.4 6.3 %collective-permute-start.4 = (bf16[40,1792]{1,0:T(8,128)(2,1)S(1)}, bf16[40,1792]{1,0:T(8,128)(2,1)S(1)}, u32[]{:S(2)}, u32[]{:S(2)}) collective-permute-start(bf16[40,1792]{1,0:T(8,128)(2,1)S(1)} %far_project.3), channel_id=1, source_target_pairs={{0,2},{1,3},{2,0},{3,1},{4,6},{5,7},{6,4},{7,5},{8,10},{9,11},{10,... | collective-permute-start | bytes 430088 | tf_op jit(solution)/shard_map/ppermute | solution.py:301

commit v4 on v2

--- a/solution.py
+++ b/solution.py
@@ -10,7 +10,7 @@
 VMEM = pl.BlockSpec(memory_space=pltpu.VMEM)
 ANY = pl.BlockSpec(memory_space=pl.ANY)
 SLAB = 128
-CUTS = (0, 5, 11, 16)
+CUTS = (0, 5, 10, 16)
 
 
 def general_body(expert_ids, gate_weights, hidden, hot_down, cold_down):
@@ -84,44 +84,45 @@
     return pltpu.make_async_copy(flat.at[pl.ds(start, rows_ref.shape[0])], rows_ref, sem)
 
 
-def take_kernel(start, hidden_ref, rows_ref, sems):
-    copy = rows_of(hidden_ref, start, rows_ref, sems.at[0])
-    copy.start()
-    copy.wait()
-
-
-def first_take_kernel(start, hidden_ref, ids_ref, weights_ref, rows_ref, gates_ref, ids, weights, sems):
-    copies = [
-        rows_of(hidden_ref, start, rows_ref, sems.at[0]),
-        pltpu.make_async_copy(ids_ref, ids, sems.at[1]),
-        pltpu.make_async_copy(weights_ref, weights, sems.at[2]),
+def take_kernel(hidden_ref, ids_ref, weights_ref, *refs):
+    *row_refs, gates_ref, ids, weights, sems = refs
+    small = [
+        pltpu.make_async_copy(ids_ref, ids, sems.at[0]),
+        pltpu.make_async_copy(weights_ref, weights, sems.at[1]),
     ]
-    for copy in copies:
+    large, at = [], 0
+    for i, rows_ref in enumerate(row_refs):
+        large.append(rows_of(hidden_ref, at, rows_ref, sems.at[2 + i]))
+        at += rows_ref.shape[0]
+    for copy in small + large:
         copy.start()
-    for copy in copies[1:]:
+    for copy in small:
         copy.wait()
     for e in range(2):
         gates_ref[2 * e : 2 * e + 2, :] = jnp.where(ids[...] == e, weights[...], 0.0)
-    copies[0].wait()
-
-
-def take(hidden, start, tokens, choice=()):
-    _, choices, depth = hidden.shape
-    shapes = [pltpu.VMEM((tokens * choices, depth), hidden.dtype)]
-    scratch = [pltpu.SemaphoreType.DMA((3,))]
-    if choice:
-        shapes.append(pltpu.VMEM((2 * choices, hidden.shape[0]), choice[1].dtype))
-        scratch = [pltpu.VMEM(c.shape, c.dtype) for c in choice] + scratch
-    return pl.pallas_call(
-        functools.partial(first_take_kernel if choice else take_kernel, start * choices),
+    for copy in large:
+        copy.wait()
+
+
+def take(hidden, ids, weights, spans):
+    tokens, choices, depth = hidden.shape
+    shapes = [pltpu.VMEM(((b - a) * choices, depth), hidden.dtype) for a, b in spans]
+    shapes.append(pltpu.VMEM((2 * choices, tokens), weights.dtype))
+    *rows, gates = pl.pallas_call(
+        take_kernel,
         name="take",
         out_shape=shapes,
-        in_specs=[ANY] * (1 + len(choice)),
+        in_specs=[ANY] * 3,
         out_specs=[VMEM] * len(shapes),
-        scratch_shapes=scratch,
+        scratch_shapes=[
+            pltpu.VMEM(ids.shape, ids.dtype),
+            pltpu.VMEM(weights.shape, weights.dtype),
+            pltpu.SemaphoreType.DMA((2 + len(spans),)),
+        ],
         compiler_params=limit(2),
         cost_estimate=pl.CostEstimate(flops=0, bytes_accessed=4 * tokens * choices * depth, transcendentals=0),
-    )(*in_hbm(hidden, *choice))
+    )(*in_hbm(hidden, ids, weights))
+    return rows, gates
 
 
 def choose(rows, gates):
@@ -153,9 +154,19 @@
         yield at, end, terms[0] + terms[1]
 
 
-def far_kernel(start, rows_ref, gates_ref, c0, h0, c1, h1, out_ref):
+def far_kernel(start, part_ref, whole_ref, gates_ref, c0, h0, c1, h1, out_ref, rows):
     tokens, width = out_ref.shape[0], c0.shape[1]
-    chosen, scales = choose(rows_ref[...], columns_of(gates_ref)[start : start + tokens, :])
+    core = lax.axis_index("expert") % 2
+
+    @pl.when(core == 0)
+    def _():
+        rows[...] = part_ref[...]
+
+    @pl.when(core == 1)
+    def _():
+        rows[...] = whole_ref[start : start + tokens].reshape(rows.shape)
+
+    chosen, scales = choose(rows[...], columns_of(gates_ref)[start : start + tokens, :])
     for i, weights in enumerate(((c0, h0), (c1, h1))):
         for at, end, block in gated(chosen, scales, weights):
             out_ref[:, i * width + at : i * width + end] = block.astype(out_ref.dtype)
@@ -167,57 +178,89 @@
     )
 
 
-def far_project(start, tokens, rows, gates, own, partner):
+def far_project(start, tokens, part, whole, gates, own, partner):
     width = own[0].shape[1]
+    operands = [part, whole, gates, *own, *partner]
     return pl.pallas_call(
         functools.partial(far_kernel, start),
         name="far_project",
-        out_shape=pltpu.VMEM((tokens, 2 * width), rows.dtype),
-        in_specs=[VMEM] * 6,
+        out_shape=pltpu.VMEM((tokens, 2 * width), part.dtype),
+        in_specs=[VMEM] * len(operands),
         out_specs=VMEM,
+        scratch_shapes=[pltpu.VMEM(part.shape, part.dtype)],
         compiler_params=limit(12),
-        cost_estimate=cost_of(rows, width),
-    )(*near_core(rows, gates, *own, *partner))
-
-
-def own_kernel(*refs):
-    *row_refs, gates_ref, c0, h0, c1, h1, out_ref, staged, sems = refs
-    width = c0.shape[1]
+        cost_estimate=cost_of(part, width),
+    )(*near_core(*operands))
+
+
+def own_kernel(blocks, count, *refs):
+    row_refs, rest = refs[:count], refs[count:]
+    gates_ref, *weight_refs, whole_ref, out_ref, staged, sems = rest
+    del whole_ref
+    width = weight_refs[0].shape[1]
     me = lax.axis_index("expert")
-    gates = columns_of(gates_ref)
-    chosen, scales, at = [], [], 0
-    for rows_ref in row_refs:
-        tokens = rows_ref.shape[0] // 2
-        x, g = choose(rows_ref[...], gates[at : at + tokens, :])
-        chosen.append(x)
-        scales.append(g)
-        at += tokens
-    chosen = [jnp.concatenate(x, axis=0) for x in zip(*chosen)]
-    scales = [jnp.concatenate(g, axis=0) for g in zip(*scales)]
-    copies = []
-    for i, weights in enumerate(((c0, h0), (c1, h1))):
-        for at, end, block in gated(chosen, scales, weights):
-            staged[i, :, at:end] = block.astype(staged.dtype)
-        to = pl.multiple_of((me ^ i) * width, width)
-        copies.append(pltpu.make_async_copy(staged.at[i], out_ref.at[:, pl.ds(to, width)], sems.at[i]))
-        copies[-1].start()
-    for copy in copies:
-        copy.wait()
-
-
-def own_project(devices, rows, gates, own, partner):
-    width = own[0].shape[1]
+
+    def write(names):
+        gates = columns_of(gates_ref)
+        chosen, scales, at = [], [], 0
+        for rows_ref in row_refs:
+            tokens = rows_ref.shape[0] // 2
+            x, g = choose(rows_ref[...], gates[at : at + tokens, :])
+            chosen.append(x)
+            scales.append(g)
+            at += tokens
+        joined = [jnp.concatenate(x, axis=0) for x in zip(*chosen)]
+        spread = [jnp.concatenate(g, axis=0) for g in zip(*scales)]
+        copies = []
+        for name in names:
+            slot = [b for b, _ in blocks].index(name)
+            for at, end, block in gated(joined, spread, weight_refs[2 * slot : 2 * slot + 2]):
+                staged[name, :, at:end] = block.astype(staged.dtype)
+            to = pl.multiple_of((me ^ name) * width, width)
+            copies.append(pltpu.make_async_copy(staged.at[name], out_ref.at[:, pl.ds(to, width)], sems.at[name]))
+            copies[-1].start()
+        for copy in copies:
+            copy.wait()
+
+    if all(len(turns) == 2 for _, turns in blocks):
+        write([name for name, _ in blocks])
+        return
+    for turn in range(2):
+        names = [name for name, turns in blocks if turn in turns]
+        if names:
+            pl.when(me % 2 == turn)(functools.partial(write, names))
+
+
+def own_project(blocks, rows, gates, weights, out):
+    width = weights[0].shape[1]
     tokens = sum(r.shape[0] for r in rows) // 2
-    return pl.pallas_call(
-        own_kernel,
+    operands = [*rows, gates, *weights]
+    return pl.pallas_call(
+        functools.partial(own_kernel, blocks, len(rows)),
         name="own_project",
-        out_shape=pltpu.HBM((tokens, devices * width), rows[0].dtype),
-        in_specs=[VMEM] * (len(rows) + 5),
+        out_shape=pltpu.HBM(out.shape, out.dtype),
+        in_specs=[VMEM] * len(operands) + [ANY],
         out_specs=ANY,
         scratch_shapes=[pltpu.VMEM((2, tokens, width), rows[0].dtype), pltpu.SemaphoreType.DMA((2,))],
+        input_output_aliases={len(operands): 0},
         compiler_params=limit(12),
-        cost_estimate=cost_of(rows[0], len(rows) * width),
-    )(*near_core(*rows, gates, *own, *partner))
+        cost_estimate=cost_of(rows[0], len(rows) * width * len(weights) // 4),
+    )(*near_core(*operands), *in_hbm(out))
+
+
+def fresh_kernel(out_ref):
+    del out_ref
+
+
+def fresh(shape, dtype):
+    return pl.pallas_call(
+        fresh_kernel,
+        name="fresh",
+        out_shape=pltpu.HBM(shape, dtype),
+        out_specs=ANY,
+        compiler_params=limit(2),
+        cost_estimate=pl.CostEstimate(flops=0, bytes_accessed=0, transcendentals=0),
+    )()
 
 
 def put_kernel(start, block_ref, whole_ref, out_ref, sems):
@@ -278,32 +321,36 @@
 
 
 def pair_body(expert_ids, gate_weights, hidden, hot_down, cold_down):
-    devices = lax.axis_size("expert")
+    devices, groups = lax.axis_size("expert"), lax.axis_size("dp")
     near = [(i, i ^ 1) for i in range(devices)]
     far = [(i, i ^ 2) for i in range(devices)]
-    tokens, _, _ = hidden.shape
+    tokens = hidden.shape[0]
     cuts = [tokens * c // 16 for c in CUTS]
     spans = list(zip(cuts[:-1], cuts[1:]))
 
     def send(array, pairs):
         return lax.ppermute(array, "expert", pairs)
 
-    held, moved, source = [], [], hidden
-    for i, (a, b) in enumerate(spans):
-        if i == 0:
-            rows, gates = take(source, a, b - a, (expert_ids.T, gate_weights.T))
-        else:
-            (rows,) = take(source, a, b - a)
-        held.append(rows)
-        moved.append(send(rows, far))
+    def send_by(array, core):
+        pairs = [
+            (g * devices + i, g * devices + (i ^ 2) if i % 2 == core else (g ^ (1 + core)) * devices + i)
+            for g in range(groups)
+            for i in range(devices)
+        ]
+        return lax.ppermute(array, ("dp", "expert"), pairs)
+
+    whole = send_by(hidden, 1)
+    held, gates = take(hidden, expert_ids.T, gate_weights.T, spans)
+    moved = [send_by(rows, 0) for rows in held]
     far_gates = send(gates, far)
     partner = (send(cold_down, near), send(hot_down, near))
+    out = fresh((tokens, devices * hot_down.shape[1]), hidden.dtype)
     own = hold(cold_down, hot_down)
     back = []
     for i, (a, b) in enumerate(spans):
-        result = far_project(a, b - a, moved[i], far_gates, own, partner)
+        result = far_project(a, b - a, moved[i], whole, far_gates, own, partner)
         back.append(send(result, far))
-    out = own_project(devices, held, gates, own, partner)
+    out = own_project(((0, (0, 1)), (1, (0, 1))), held, gates, (*own, *partner), out)
     for i, (a, _) in enumerate(spans):
         out = put(a, back[i], out)
     return out
@@ -324,6 +371,6 @@
             body, mesh=mesh, in_specs=specs, out_specs=P(("dp", "expert"), None), check_vma=False
         )
 
-    if devices != 4:
+    if devices != 4 or mesh.shape["dp"] % 4:
         return spread(general_body)
     return spread(pair_body)

time: 30.6 us -> 31.5 us (1.029)
  starting transfers between devices: 9.88 us -> 11.6 us
  Pallas kernels: 14.5 us -> 12.8 us
  waiting for transfers between devices: 5.97 us -> 6.77 us
    ppermute x0 -> x4, starting transfers between devices: none -> 6.63 us  [send_by(): return lax.ppermute(array, ('dp', 'expert'), pairs)]
    ppermute x9 -> x6, starting transfers between devices: 9.88 us -> 5.01 us  [send(): return lax.ppermute(array, 'expert', pairs)]
    pallas_call x4 -> x3, Pallas kernels: 6.11 us -> 4.4 us  [the longest x1 3.25 us: own_project(): pl.pallas_call(functools.partial(own_kernel, blocks, len(rows)), name='ow...]
    ppermute x9 -> x6, waiting for transfers between devices: 5.97 us -> 6.76 us  [send(): return lax.ppermute(array, 'expert', pairs)]
  transfers between devices with their start and end apart: 9 -> 10, of which waited for: 3 -> 2; matrix products, arithmetic and copies ran while one was open for 0% -> 0% of each run, Pallas kernels for 45% -> 39%
where the time goes in v4:
time: 31.5 us; the launch traced here: 31.4 us
  Pallas kernels  12.8 us (41%)
  starting transfers between devices  11.6 us (37%)
  waiting for transfers between devices  6.77 us (21%)
    ppermute x6, waiting for transfers between devices, send(): return lax.ppermute(array, 'expert', pairs)  6.76 us
    ppermute x4, starting transfers between devices, send_by(): return lax.ppermute(array, ('dp', 'expert'), pairs)  6.63 us
    ppermute x6, starting transfers between devices, send(): return lax.ppermute(array, 'expert', pairs)  5.01 us
    pallas_call x3, Pallas kernels, far_project(): pl.pallas_call(functools.partial(far_kernel, start), name='far_project',...  4.32 us
    pallas_call x1, Pallas kernels, own_project(): pl.pallas_call(functools.partial(own_kernel, blocks, len(rows)), name='ow...  3.25 us
    pallas_call x1, Pallas kernels, hold(): pl.pallas_call(hold_kernel, name='hold', out_shape=[pltpu.VMEM(a.shape, a...  2.07 us
    pallas_call x3, Pallas kernels, put(): pl.pallas_call(functools.partial(put_kernel, start), name='put', out_shap...  2.05 us
    pallas_call x1, Pallas kernels, take(): pl.pallas_call(take_kernel, name='take', out_shape=shapes, in_specs=[ANY]...  1.16 us
  transfers between devices with their start and end apart: 10, of which 2 were waited for; matrix products, arithmetic and copies ran while one was open for 0% of the time, Pallas kernels for 39%

profile of v4, /device:TPU:0, one launch (start us, length us, event | category | flops | bytes accessed | tf_op | source)
XLA Modules:
  0.0 31.4 jit_solution(15634833527609725486)
XLA Ops:
  0.0 0.5 %collective-permute-start.3 = (bf16[1024,896]{1,0:T(8,128)(2,1)}, bf16[1024,896]{1,0:T(8,128)(2,1)S(1)}, u32[]{:S(2)}, u32[]{:S(2)}) collective-permute-start(bf16[1024,896]{1,0:T(8,128)(2,1)} %refs_0_.1), channel_id=1, source_target_pairs={{0,1},{1,0},{2,3},{3,2},{4,5},{5,4},{6,7},{7,6},{8,9},{9,8},{10,11... | collective-permute-start | bytes 5505032 | tf_op jit(solution)/shard_map/ppermute | solution.py:332
  0.5 0.0 collective-permute-start.4
  0.5 3.1 %collective-permute-start.1 = (bf16[128,2,1024]{2,1,0:T(2,128)(2,1)}, bf16[128,2,1024]{2,1,0:T(2,128)(2,1)S(1)}, u32[]{:S(2)}, u32[]{:S(2)}) collective-permute-start(bf16[128,2,1024]{2,1,0:T(2,128)(2,1)} %hidden_ref.1), channel_id=1, source_target_pairs={{0,8},{1,3},{2,10},{3,1},{4,12},{5,7},{6,14},{7,5},{8,0},{9,11},{1... | collective-permute-start | bytes 1572872 | tf_op jit(solution)/shard_map/ppermute | solution.py:340
  3.6 1.2 %take.1 = (bf16[80,1024]{1,0:T(8,128)(2,1)S(1)}, bf16[80,1024]{1,0:T(8,128)(2,1)S(1)}, bf16[96,1024]{1,0:T(8,128)(2,1)S(1)}, f32[4,128]{1,0:T(4,128)S(1)}) custom-call(bf16[128,2,1024]{2,1,0:T(2,128)(2,1)} %hidden_ref.1, s32[2,128]{1,0:T(2,128)} %bitcast.2, f32[2,128]{1,0:T(2,128)} %bitcast.3), custom_call_target="tpu_custom_call" | custom-call | bytes 1048576 | tf_op jit(solution)/shard_map/take/pallas_call | solution.py:111
  4.7 1.6 %collective-permute-start = (bf16[96,1024]{1,0:T(8,128)(2,1)S(1)}, bf16[96,1024]{1,0:T(8,128)(2,1)S(1)}, u32[]{:S(2)}, u32[]{:S(2)}) collective-permute-start(bf16[96,1024]{1,0:T(8,128)(2,1)S(1)} %get-tuple-element.11.refs_2_), channel_id=1, source_target_pairs={{0,2},{1,5},{2,0},{3,7},{4,6},{5,1},{6,4},{7,3},{8,10},{9,13},{10,... | collective-permute-start | bytes 589832 | tf_op jit(solution)/shard_map/ppermute | solution.py:340
  6.3 0.5 %collective-permute-start.2 = (f32[4,128]{1,0:T(4,128)S(1)}, f32[4,128]{1,0:T(4,128)S(1)}, u32[]{:S(2)}, u32[]{:S(2)}) collective-permute-start(f32[4,128]{1,0:T(4,128)S(1)} %get-tuple-element.12.refs_3_), channel_id=1, source_target_pairs={{0,2},{1,3},{2,0},{3,1},{4,6},{5,7},{6,4},{7,5},{8,10},{9,11},{10,... | collective-permute-start | bytes 6152 | tf_op jit(solution)/shard_map/ppermute | solution.py:332
  6.8 5.5 %collective-permute-done.2.gates_ref = f32[4,128]{1,0:T(4,128)S(1)} collective-permute-done((f32[4,128]{1,0:T(4,128)S(1)}, f32[4,128]{1,0:T(4,128)S(1)}, u32[]{:S(2)}, u32[]{:S(2)}) %collective-permute-start.2) | collective-permute-done | bytes 2080 | tf_op jit(solution)/shard_map/ppermute | solution.py:332
  12.3 1.7 %collective-permute-start.8 = (bf16[80,1024]{1,0:T(8,128)(2,1)S(1)}, bf16[80,1024]{1,0:T(8,128)(2,1)S(1)}, u32[]{:S(2)}, u32[]{:S(2)}) collective-permute-start(bf16[80,1024]{1,0:T(8,128)(2,1)S(1)} %get-tuple-element.16.refs_0_), channel_id=1, source_target_pairs={{0,2},{1,5},{2,0},{3,7},{4,6},{5,1},{6,4},{7,3},{8,10},{9,13},{10,... | collective-permute-start | bytes 491528 | tf_op jit(solution)/shard_map/ppermute | solution.py:340
  14.1 0.3 collective-permute-start.6
  14.3 2.1 %hold.1 = (bf16[1024,896]{1,0:T(8,128)(2,1)S(1)}, bf16[1024,896]{1,0:T(8,128)(2,1)S(1)}) custom-call(bf16[1024,896]{1,0:T(8,128)(2,1)} %refs_0_.1, bf16[1024,896]{1,0:T(8,128)(2,1)} %refs_1_.1), custom_call_target="tpu_custom_call" | custom-call | bytes 7340032 | tf_op jit(solution)/shard_map/hold/pallas_call | solution.py:309
  16.4 0.0 collective-permute-done.1.whole_ref
  16.4 1.5 %far_project.3 = bf16[48,1792]{1,0:T(8,128)(2,1)S(1)} custom-call(bf16[96,1024]{1,0:T(8,128)(2,1)S(1)} %collective-permute-done.part_ref, bf16[128,2,1024]{2,1,0:T(2,128)(2,1)S(1)} %collective-permute-done.1.whole_ref, f32[4,128]{1,0:T(4,128)S(1)} %collective-permute-done.2.gates_ref, bf16[1024,896]{1,0:T(8,128)(2,1)S(1)} %get-tuple-element.13.c0.refs_4_, ...), custom_call_target="tpu_custom_call" | custom-call | flops 352321536 | bytes 688128 | tf_op jit(solution)/shard_map/far_project/pallas_call | solution.py:184
  17.9 1.8 %collective-permute-start.5 = (bf16[48,1792]{1,0:T(8,128)(2,1)S(1)}, bf16[48,1792]{1,0:T(8,128)(2,1)S(1)}, u32[]{:S(2)}, u32[]{:S(2)}) collective-permute-start(bf16[48,1792]{1,0:T(8,128)(2,1)S(1)} %far_project.3), channel_id=1, source_target_pairs={{0,2},{1,3},{2,0},{3,1},{4,6},{5,7},{6,4},{7,5},{8,10},{9,11},{10,... | collective-permute-start | bytes 516104 | tf_op jit(solution)/shard_map/ppermute | solution.py:332
  19.7 0.0 collective-permute-done.8.part_ref
  19.7 1.4 %far_project.5 = bf16[40,1792]{1,0:T(8,128)(2,1)S(1)} custom-call(bf16[80,1024]{1,0:T(8,128)(2,1)S(1)} %collective-permute-done.8.part_ref, bf16[128,2,1024]{2,1,0:T(2,128)(2,1)S(1)} %collective-permute-done.1.whole_ref, f32[4,128]{1,0:T(4,128)S(1)} %collective-permute-done.2.gates_ref, bf16[1024,896]{1,0:T(8,128)(2,1)S(1)} %get-tuple-element.13.c0.refs_4_, ...), custom_call_target="tpu_custom_call" | custom-call | flops 293601280 | bytes 573440 | tf_op jit(solution)/shard_map/far_project/pallas_call | solution.py:184
  21.2 0.3 %collective-permute-start.9 = (bf16[40,1792]{1,0:T(8,128)(2,1)S(1)}, bf16[40,1792]{1,0:T(8,128)(2,1)S(1)}, u32[]{:S(2)}, u32[]{:S(2)}) collective-permute-start(bf16[40,1792]{1,0:T(8,128)(2,1)S(1)} %far_project.5), channel_id=1, source_target_pairs={{0,2},{1,3},{2,0},{3,1},{4,6},{5,7},{6,4},{7,5},{8,10},{9,11},{10,... | collective-permute-start | bytes 430088 | tf_op jit(solution)/shard_map/ppermute | solution.py:332
  21.5 0.0 collective-permute-done.6.part_ref
  21.5 1.4 %far_project.4 = bf16[40,1792]{1,0:T(8,128)(2,1)S(1)} custom-call(bf16[80,1024]{1,0:T(8,128)(2,1)S(1)} %collective-permute-done.6.part_ref, bf16[128,2,1024]{2,1,0:T(2,128)(2,1)S(1)} %collective-permute-done.1.whole_ref, f32[4,128]{1,0:T(4,128)S(1)} %collective-permute-done.2.gates_ref, bf16[1024,896]{1,0:T(8,128)(2,1)S(1)} %get-tuple-element.13.c0.refs_4_, ...), custom_call_target="tpu_custom_call" | custom-call | flops 293601280 | bytes 573440 | tf_op jit(solution)/shard_map/far_project/pallas_call | solution.py:184
  23.0 1.8 %collective-permute-start.7 = (bf16[40,1792]{1,0:T(8,128)(2,1)S(1)}, bf16[40,1792]{1,0:T(8,128)(2,1)S(1)}, u32[]{:S(2)}, u32[]{:S(2)}) collective-permute-start(bf16[40,1792]{1,0:T(8,128)(2,1)S(1)} %far_project.4), channel_id=1, source_target_pairs={{0,2},{1,3},{2,0},{3,1},{4,6},{5,7},{6,4},{7,5},{8,10},{9,11},{10,... | collective-permute-start | bytes 430088 | tf_op jit(solution)/shard_map/ppermute | solution.py:332
  24.8 3.2 %own_project.1.whole_ref = bf16[128,3584]{1,0:T(8,128)(2,1)} custom-call(bf16[80,1024]{1,0:T(8,128)(2,1)S(1)} %get-tuple-element.16.refs_0_, bf16[80,1024]{1,0:T(8,128)(2,1)S(1)} %get-tuple-element.15.refs_1_, bf16[96,1024]{1,0:T(8,128)(2,1)S(1)} %get-tuple-element.11.refs_2_, ...), custom_call_target="tpu_custom_call", output_to_operand_aliasing={{}: (8, {})} | custom-call | flops 880803840 | bytes 1720320 | tf_op jit(solution)/shard_map/own_project/pallas_call | solution.py:238
  28.0 0.7 %put.3.whole_ref = bf16[128,3584]{1,0:T(8,128)(2,1)} custom-call(bf16[40,1792]{1,0:T(8,128)(2,1)S(1)} %collective-permute-done.9.block_ref, bf16[128,3584]{1,0:T(8,128)(2,1)} %own_project.1.whole_ref), custom_call_target="tpu_custom_call", output_to_operand_aliasing={{}: (1, {})} | custom-call | bytes 286720 | tf_op jit(solution)/shard_map/put/pallas_call | solution.py:286
  28.7 1.3 %collective-permute-done.7.block_ref = bf16[40,1792]{1,0:T(8,128)(2,1)S(1)} collective-permute-done((bf16[40,1792]{1,0:T(8,128)(2,1)S(1)}, bf16[40,1792]{1,0:T(8,128)(2,1)S(1)}, u32[]{:S(2)}, u32[]{:S(2)}) %collective-permute-start.7) | collective-permute-done | bytes 143392 | tf_op jit(solution)/shard_map/ppermute | solution.py:332
  30.0 0.7 %put.4.whole_ref = bf16[128,3584]{1,0:T(8,128)(2,1)} custom-call(bf16[40,1792]{1,0:T(8,128)(2,1)S(1)} %collective-permute-done.7.block_ref, bf16[128,3584]{1,0:T(8,128)(2,1)} %put.3.whole_ref), custom_call_target="tpu_custom_call", output_to_operand_aliasing={{}: (1, {})} | custom-call | bytes 286720 | tf_op jit(solution)/shard_map/put/pallas_call | solution.py:286
  30.7 0.7 %put.5 = bf16[128,3584]{1,0:T(8,128)(2,1)} custom-call(bf16[48,1792]{1,0:T(8,128)(2,1)S(1)} %collective-permute-done.5.block_ref, bf16[128,3584]{1,0:T(8,128)(2,1)} %put.4.whole_ref), custom_call_target="tpu_custom_call", output_to_operand_aliasing={{}: (1, {})} | custom-call | bytes 344064 | tf_op jit(solution)/shard_map/put/pallas_call | solution.py:286
  (6 shorter events, 0.0 us)
Async XLA Ops:
  0.0 16.4 %collective-permute-start.3 = (bf16[1024,896]{1,0:T(8,128)(2,1)}, bf16[1024,896]{1,0:T(8,128)(2,1)S(1)}, u32[]{:S(2)}, u32[]{:S(2)}) collective-permute-start(bf16[1024,896]{1,0:T(8,128)(2,1)} %refs_0_.1), channel_id=1, source_target_pairs={{0,1},{1,0},{2,3},{3,2},{4,5},{5,4},{6,7},{7,6},{8,9},{9,8},{10,11... | collective-permute-start | bytes 5505032 | tf_op jit(solution)/shard_map/ppermute | solution.py:332
  0.5 15.9 %collective-permute-start.4 = (bf16[1024,896]{1,0:T(8,128)(2,1)}, bf16[1024,896]{1,0:T(8,128)(2,1)S(1)}, u32[]{:S(2)}, u32[]{:S(2)}) collective-permute-start(bf16[1024,896]{1,0:T(8,128)(2,1)} %refs_1_.1), channel_id=1, source_target_pairs={{0,1},{1,0},{2,3},{3,2},{4,5},{5,4},{6,7},{7,6},{8,9},{9,8},{10,11... | collective-permute-start | bytes 5505032 | tf_op jit(solution)/shard_map/ppermute | solution.py:332
  0.5 15.9 %collective-permute-start.1 = (bf16[128,2,1024]{2,1,0:T(2,128)(2,1)}, bf16[128,2,1024]{2,1,0:T(2,128)(2,1)S(1)}, u32[]{:S(2)}, u32[]{:S(2)}) collective-permute-start(bf16[128,2,1024]{2,1,0:T(2,128)(2,1)} %hidden_ref.1), channel_id=1, source_target_pairs={{0,8},{1,3},{2,10},{3,1},{4,12},{5,7},{6,14},{7,5},{8,0},{9,11},{1... | collective-permute-start | bytes 1572872 | tf_op jit(solution)/shard_map/ppermute | solution.py:340
  4.7 9.3 %collective-permute-start = (bf16[96,1024]{1,0:T(8,128)(2,1)S(1)}, bf16[96,1024]{1,0:T(8,128)(2,1)S(1)}, u32[]{:S(2)}, u32[]{:S(2)}) collective-permute-start(bf16[96,1024]{1,0:T(8,128)(2,1)S(1)} %get-tuple-element.11.refs_2_), channel_id=1, source_target_pairs={{0,2},{1,5},{2,0},{3,7},{4,6},{5,1},{6,4},{7,3},{8,10},{9,13},{10,... | collective-permute-start | bytes 589832 | tf_op jit(solution)/shard_map/ppermute | solution.py:340
  6.3 6.0 %collective-permute-start.2 = (f32[4,128]{1,0:T(4,128)S(1)}, f32[4,128]{1,0:T(4,128)S(1)}, u32[]{:S(2)}, u32[]{:S(2)}) collective-permute-start(f32[4,128]{1,0:T(4,128)S(1)} %get-tuple-element.12.refs_3_), channel_id=1, source_target_pairs={{0,2},{1,3},{2,0},{3,1},{4,6},{5,7},{6,4},{7,5},{8,10},{9,11},{10,... | collective-permute-start | bytes 6152 | tf_op jit(solution)/shard_map/ppermute | solution.py:332
  12.3 7.4 %collective-permute-start.8 = (bf16[80,1024]{1,0:T(8,128)(2,1)S(1)}, bf16[80,1024]{1,0:T(8,128)(2,1)S(1)}, u32[]{:S(2)}, u32[]{:S(2)}) collective-permute-start(bf16[80,1024]{1,0:T(8,128)(2,1)S(1)} %get-tuple-element.16.refs_0_), channel_id=1, source_target_pairs={{0,2},{1,5},{2,0},{3,7},{4,6},{5,1},{6,4},{7,3},{8,10},{9,13},{10,... | collective-permute-start | bytes 491528 | tf_op jit(solution)/shard_map/ppermute | solution.py:340
  14.1 7.5 %collective-permute-start.6 = (bf16[80,1024]{1,0:T(8,128)(2,1)S(1)}, bf16[80,1024]{1,0:T(8,128)(2,1)S(1)}, u32[]{:S(2)}, u32[]{:S(2)}) collective-permute-start(bf16[80,1024]{1,0:T(8,128)(2,1)S(1)} %get-tuple-element.15.refs_1_), channel_id=1, source_target_pairs={{0,2},{1,5},{2,0},{3,7},{4,6},{5,1},{6,4},{7,3},{8,10},{9,13},{10,... | collective-permute-start | bytes 491528 | tf_op jit(solution)/shard_map/ppermute | solution.py:340
  17.9 12.7 %collective-permute-start.5 = (bf16[48,1792]{1,0:T(8,128)(2,1)S(1)}, bf16[48,1792]{1,0:T(8,128)(2,1)S(1)}, u32[]{:S(2)}, u32[]{:S(2)}) collective-permute-start(bf16[48,1792]{1,0:T(8,128)(2,1)S(1)} %far_project.3), channel_id=1, source_target_pairs={{0,2},{1,3},{2,0},{3,1},{4,6},{5,7},{6,4},{7,5},{8,10},{9,11},{10,... | collective-permute-start | bytes 516104 | tf_op jit(solution)/shard_map/ppermute | solution.py:332
  21.2 6.9 %collective-permute-start.9 = (bf16[40,1792]{1,0:T(8,128)(2,1)S(1)}, bf16[40,1792]{1,0:T(8,128)(2,1)S(1)}, u32[]{:S(2)}, u32[]{:S(2)}) collective-permute-start(bf16[40,1792]{1,0:T(8,128)(2,1)S(1)} %far_project.5), channel_id=1, source_target_pairs={{0,2},{1,3},{2,0},{3,1},{4,6},{5,7},{6,4},{7,5},{8,10},{9,11},{10,... | collective-permute-start | bytes 430088 | tf_op jit(solution)/shard_map/ppermute | solution.py:332
  23.0 7.0 %collective-permute-start.7 = (bf16[40,1792]{1,0:T(8,128)(2,1)S(1)}, bf16[40,1792]{1,0:T(8,128)(2,1)S(1)}, u32[]{:S(2)}, u32[]{:S(2)}) collective-permute-start(bf16[40,1792]{1,0:T(8,128)(2,1)S(1)} %far_project.4), channel_id=1, source_target_pairs={{0,2},{1,3},{2,0},{3,1},{4,6},{5,7},{6,4},{7,5},{8,10},{9,11},{10,... | collective-permute-start | bytes 430088 | tf_op jit(solution)/shard_map/ppermute | solution.py:332

commit v5 on v4

--- a/solution.py
+++ b/solution.py
@@ -263,37 +263,41 @@
     )()
 
 
-def put_kernel(start, block_ref, whole_ref, out_ref, sems):
-    del whole_ref
-    tokens, width = block_ref.shape[0], block_ref.shape[1] // 2
+def put_kernel(starts, *refs):
+    block_refs, (_, out_ref, sems) = refs[: len(starts)], refs[len(starts) :]
     me = lax.axis_index("expert")
     copies = []
-    for i in range(2):
-        to = pl.multiple_of((me ^ 2 ^ i) * width, width)
-        copies.append(
-            pltpu.make_async_copy(
-                block_ref.at[:, pl.ds(i * width, width)],
-                out_ref.at[pl.ds(start, tokens), pl.ds(to, width)],
-                sems.at[i],
+    for start, block_ref in zip(starts, block_refs):
+        tokens, width = block_ref.shape[0], block_ref.shape[1] // 2
+        for i in range(2):
+            to = pl.multiple_of((me ^ 2 ^ i) * width, width)
+            copies.append(
+                pltpu.make_async_copy(
+                    block_ref.at[:, pl.ds(i * width, width)],
+                    out_ref.at[pl.ds(start, tokens), pl.ds(to, width)],
+                    sems.at[len(copies)],
+                )
             )
-        )
-        copies[-1].start()
+            copies[-1].start()
     for copy in copies:
         copy.wait()
 
 
-def put(start, block, whole):
-    return pl.pallas_call(
-        functools.partial(put_kernel, start),
+def put(starts, blocks, whole):
+    count = len(starts)
+    return pl.pallas_call(
+        functools.partial(put_kernel, starts),
         name="put",
         out_shape=pltpu.HBM(whole.shape, whole.dtype),
-        in_specs=[VMEM, ANY],
+        in_specs=[VMEM] * count + [ANY],
         out_specs=ANY,
-        scratch_shapes=[pltpu.SemaphoreType.DMA((2,))],
-        input_output_aliases={1: 0},
+        scratch_shapes=[pltpu.SemaphoreType.DMA((2 * count,))],
+        input_output_aliases={count: 0},
         compiler_params=limit(2),
-        cost_estimate=pl.CostEstimate(flops=0, bytes_accessed=4 * block.size, transcendentals=0),
-    )(*near_core(block), *in_hbm(whole))
+        cost_estimate=pl.CostEstimate(
+            flops=0, bytes_accessed=4 * sum(b.size for b in blocks), transcendentals=0
+        ),
+    )(*near_core(*blocks), *in_hbm(whole))
 
 
 def hold_kernel(*refs):
@@ -348,11 +352,14 @@
     own = hold(cold_down, hot_down)
     back = []
     for i, (a, b) in enumerate(spans):
+        if i == 2:
+            out = own_project(((0, (1,)),), held, gates, own, out)
         result = far_project(a, b - a, moved[i], whole, far_gates, own, partner)
         back.append(send(result, far))
-    out = own_project(((0, (0, 1)), (1, (0, 1))), held, gates, (*own, *partner), out)
-    for i, (a, _) in enumerate(spans):
-        out = put(a, back[i], out)
+    out = own_project(((0, (0,)), (1, (0, 1))), held, gates, (*own, *partner), out)
+    starts = [a for a, _ in spans]
+    out = put(starts[:-1], back[:-1], out)
+    out = put(starts[-1:], back[-1:], out)
     return out
 
 

time: 31.5 us -> 31.6 us (level)
  waiting for transfers between devices: 6.77 us -> 7.42 us
  Pallas kernels: 12.8 us -> 12.2 us
    ppermute x6, waiting for transfers between devices: 6.76 us -> 7.41 us  [send(): return lax.ppermute(array, 'expert', pairs)]
    pallas_call x3 -> x2, Pallas kernels: 2.05 us -> 1.43 us  [put(): pl.pallas_call(functools.partial(put_kernel, starts), name='put', out_sha...]
    pallas_call x1 -> x2, Pallas kernels: 3.25 us -> 3.28 us  [own_project(): pl.pallas_call(functools.partial(own_kernel, blocks, len(rows)), name='ow...]
  transfers between devices with their start and end apart: 10 -> 10, of which waited for: 2 -> 2; matrix products, arithmetic and copies ran while one was open for 0% -> 0% of each run, Pallas kernels for 39% -> 37%
where the time goes in v5:
time: 31.6 us; the launch traced here: 31.4 us
  Pallas kernels  12.2 us (39%)
  starting transfers between devices  11.6 us (37%)
  waiting for transfers between devices  7.42 us (23%)
    ppermute x6, waiting for transfers between devices, send(): return lax.ppermute(array, 'expert', pairs)  7.41 us
    ppermute x4, starting transfers between devices, send_by(): return lax.ppermute(array, ('dp', 'expert'), pairs)  6.63 us
    ppermute x6, starting transfers between devices, send(): return lax.ppermute(array, 'expert', pairs)  5.01 us
    pallas_call x3, Pallas kernels, far_project(): pl.pallas_call(functools.partial(far_kernel, start), name='far_project',...  4.31 us
    pallas_call x2, Pallas kernels, own_project(): pl.pallas_call(functools.partial(own_kernel, blocks, len(rows)), name='ow...  3.28 us
    pallas_call x1, Pallas kernels, hold(): pl.pallas_call(hold_kernel, name='hold', out_shape=[pltpu.VMEM(a.shape, a...  2.07 us
    pallas_call x2, Pallas kernels, put(): pl.pallas_call(functools.partial(put_kernel, starts), name='put', out_sha...  1.43 us
    pallas_call x1, Pallas kernels, take(): pl.pallas_call(take_kernel, name='take', out_shape=shapes, in_specs=[ANY]...  1.16 us
  transfers between devices with their start and end apart: 10, of which 2 were waited for; matrix products, arithmetic and copies ran while one was open for 0% of the time, Pallas kernels for 37%

profile of v5, /device:TPU:0, one launch (start us, length us, event | category | flops | bytes accessed | tf_op | source)
XLA Modules:
  0.0 31.4 jit_solution(210319667641408447)
XLA Ops:
  0.0 0.5 %collective-permute-start.4 = (bf16[1024,896]{1,0:T(8,128)(2,1)}, bf16[1024,896]{1,0:T(8,128)(2,1)S(1)}, u32[]{:S(2)}, u32[]{:S(2)}) collective-permute-start(bf16[1024,896]{1,0:T(8,128)(2,1)} %refs_1_.1), channel_id=1, source_target_pairs={{0,1},{1,0},{2,3},{3,2},{4,5},{5,4},{6,7},{7,6},{8,9},{9,8},{10,11... | collective-permute-start | bytes 5505032 | tf_op jit(solution)/shard_map/ppermute | solution.py:336
  0.5 0.0 collective-permute-start.3
  0.5 3.1 %collective-permute-start.1 = (bf16[128,2,1024]{2,1,0:T(2,128)(2,1)}, bf16[128,2,1024]{2,1,0:T(2,128)(2,1)S(1)}, u32[]{:S(2)}, u32[]{:S(2)}) collective-permute-start(bf16[128,2,1024]{2,1,0:T(2,128)(2,1)} %hidden_ref.1), channel_id=1, source_target_pairs={{0,8},{1,3},{2,10},{3,1},{4,12},{5,7},{6,14},{7,5},{8,0},{9,11},{1... | collective-permute-start | bytes 1572872 | tf_op jit(solution)/shard_map/ppermute | solution.py:344
  3.6 1.2 %take.1 = (bf16[80,1024]{1,0:T(8,128)(2,1)S(1)}, bf16[80,1024]{1,0:T(8,128)(2,1)S(1)}, bf16[96,1024]{1,0:T(8,128)(2,1)S(1)}, f32[4,128]{1,0:T(4,128)S(1)}) custom-call(bf16[128,2,1024]{2,1,0:T(2,128)(2,1)} %hidden_ref.1, s32[2,128]{1,0:T(2,128)} %bitcast.2, f32[2,128]{1,0:T(2,128)} %bitcast.3), custom_call_target="tpu_custom_call" | custom-call | bytes 1048576 | tf_op jit(solution)/shard_map/take/pallas_call | solution.py:111
  4.7 1.6 %collective-permute-start = (bf16[96,1024]{1,0:T(8,128)(2,1)S(1)}, bf16[96,1024]{1,0:T(8,128)(2,1)S(1)}, u32[]{:S(2)}, u32[]{:S(2)}) collective-permute-start(bf16[96,1024]{1,0:T(8,128)(2,1)S(1)} %get-tuple-element.11.refs_2_), channel_id=1, source_target_pairs={{0,2},{1,5},{2,0},{3,7},{4,6},{5,1},{6,4},{7,3},{8,10},{9,13},{10,... | collective-permute-start | bytes 589832 | tf_op jit(solution)/shard_map/ppermute | solution.py:344
  6.3 0.5 %collective-permute-start.2 = (f32[4,128]{1,0:T(4,128)S(1)}, f32[4,128]{1,0:T(4,128)S(1)}, u32[]{:S(2)}, u32[]{:S(2)}) collective-permute-start(f32[4,128]{1,0:T(4,128)S(1)} %get-tuple-element.12.refs_3_), channel_id=1, source_target_pairs={{0,2},{1,3},{2,0},{3,1},{4,6},{5,7},{6,4},{7,5},{8,10},{9,11},{10,... | collective-permute-start | bytes 6152 | tf_op jit(solution)/shard_map/ppermute | solution.py:336
  6.8 5.5 %collective-permute-done.2.gates_ref = f32[4,128]{1,0:T(4,128)S(1)} collective-permute-done((f32[4,128]{1,0:T(4,128)S(1)}, f32[4,128]{1,0:T(4,128)S(1)}, u32[]{:S(2)}, u32[]{:S(2)}) %collective-permute-start.2) | collective-permute-done | bytes 2080 | tf_op jit(solution)/shard_map/ppermute | solution.py:336
  12.3 1.7 %collective-permute-start.6 = (bf16[80,1024]{1,0:T(8,128)(2,1)S(1)}, bf16[80,1024]{1,0:T(8,128)(2,1)S(1)}, u32[]{:S(2)}, u32[]{:S(2)}) collective-permute-start(bf16[80,1024]{1,0:T(8,128)(2,1)S(1)} %get-tuple-element.15.refs_0_), channel_id=1, source_target_pairs={{0,2},{1,5},{2,0},{3,7},{4,6},{5,1},{6,4},{7,3},{8,10},{9,13},{10,... | collective-permute-start | bytes 491528 | tf_op jit(solution)/shard_map/ppermute | solution.py:344
  14.1 0.0 collective-permute-done.part_ref
  14.1 0.3 collective-permute-start.8
  14.3 2.1 %hold.1 = (bf16[1024,896]{1,0:T(8,128)(2,1)S(1)}, bf16[1024,896]{1,0:T(8,128)(2,1)S(1)}) custom-call(bf16[1024,896]{1,0:T(8,128)(2,1)} %refs_0_.1, bf16[1024,896]{1,0:T(8,128)(2,1)} %refs_1_.1), custom_call_target="tpu_custom_call" | custom-call | bytes 7340032 | tf_op jit(solution)/shard_map/hold/pallas_call | solution.py:313
  16.4 0.0 collective-permute-done.1.whole_ref
  16.4 0.0 collective-permute-done.4.h1.refs_7_
  16.4 1.5 %far_project.3 = bf16[48,1792]{1,0:T(8,128)(2,1)S(1)} custom-call(bf16[96,1024]{1,0:T(8,128)(2,1)S(1)} %collective-permute-done.part_ref, bf16[128,2,1024]{2,1,0:T(2,128)(2,1)S(1)} %collective-permute-done.1.whole_ref, f32[4,128]{1,0:T(4,128)S(1)} %collective-permute-done.2.gates_ref, bf16[1024,896]{1,0:T(8,128)(2,1)S(1)} %get-tuple-element.13.c0.refs_4_, ...), custom_call_target="tpu_custom_call" | custom-call | flops 352321536 | bytes 688128 | tf_op jit(solution)/shard_map/far_project/pallas_call | solution.py:184
  17.9 1.8 %collective-permute-start.5 = (bf16[48,1792]{1,0:T(8,128)(2,1)S(1)}, bf16[48,1792]{1,0:T(8,128)(2,1)S(1)}, u32[]{:S(2)}, u32[]{:S(2)}) collective-permute-start(bf16[48,1792]{1,0:T(8,128)(2,1)S(1)} %far_project.3), channel_id=1, source_target_pairs={{0,2},{1,3},{2,0},{3,1},{4,6},{5,7},{6,4},{7,5},{8,10},{9,11},{10,... | collective-permute-start | bytes 516104 | tf_op jit(solution)/shard_map/ppermute | solution.py:336
  19.7 1.4 %far_project.4 = bf16[40,1792]{1,0:T(8,128)(2,1)S(1)} custom-call(bf16[80,1024]{1,0:T(8,128)(2,1)S(1)} %collective-permute-done.6.part_ref, bf16[128,2,1024]{2,1,0:T(2,128)(2,1)S(1)} %collective-permute-done.1.whole_ref, f32[4,128]{1,0:T(4,128)S(1)} %collective-permute-done.2.gates_ref, bf16[1024,896]{1,0:T(8,128)(2,1)S(1)} %get-tuple-element.13.c0.refs_4_, ...), custom_call_target="tpu_custom_call" | custom-call | flops 293601280 | bytes 573440 | tf_op jit(solution)/shard_map/far_project/pallas_call | solution.py:184
  21.2 0.3 %collective-permute-start.7 = (bf16[40,1792]{1,0:T(8,128)(2,1)S(1)}, bf16[40,1792]{1,0:T(8,128)(2,1)S(1)}, u32[]{:S(2)}, u32[]{:S(2)}) collective-permute-start(bf16[40,1792]{1,0:T(8,128)(2,1)S(1)} %far_project.4), channel_id=1, source_target_pairs={{0,2},{1,3},{2,0},{3,1},{4,6},{5,7},{6,4},{7,5},{8,10},{9,11},{10,... | collective-permute-start | bytes 430088 | tf_op jit(solution)/shard_map/ppermute | solution.py:336
  21.5 1.4 %far_project.5 = bf16[40,1792]{1,0:T(8,128)(2,1)S(1)} custom-call(bf16[80,1024]{1,0:T(8,128)(2,1)S(1)} %collective-permute-done.8.part_ref, bf16[128,2,1024]{2,1,0:T(2,128)(2,1)S(1)} %collective-permute-done.1.whole_ref, f32[4,128]{1,0:T(4,128)S(1)} %collective-permute-done.2.gates_ref, bf16[1024,896]{1,0:T(8,128)(2,1)S(1)} %get-tuple-element.13.c0.refs_4_, ...), custom_call_target="tpu_custom_call" | custom-call | flops 293601280 | bytes 573440 | tf_op jit(solution)/shard_map/far_project/pallas_call | solution.py:184
  22.9 1.8 %collective-permute-start.9 = (bf16[40,1792]{1,0:T(8,128)(2,1)S(1)}, bf16[40,1792]{1,0:T(8,128)(2,1)S(1)}, u32[]{:S(2)}, u32[]{:S(2)}) collective-permute-start(bf16[40,1792]{1,0:T(8,128)(2,1)S(1)} %far_project.5), channel_id=1, source_target_pairs={{0,2},{1,3},{2,0},{3,1},{4,6},{5,7},{6,4},{7,5},{8,10},{9,11},{10,... | collective-permute-start | bytes 430088 | tf_op jit(solution)/shard_map/ppermute | solution.py:336
  24.8 3.3 %own_project.3.refs_2_ = bf16[128,3584]{1,0:T(8,128)(2,1)} custom-call(bf16[80,1024]{1,0:T(8,128)(2,1)S(1)} %get-tuple-element.15.refs_0_, bf16[80,1024]{1,0:T(8,128)(2,1)S(1)} %get-tuple-element.16.refs_1_, bf16[96,1024]{1,0:T(8,128)(2,1)S(1)} %get-tuple-element.11.refs_2_, f32[4,128]{1,0:T(4,128)S(1)} %get-tuple-element.12.refs_3_, ...), custom_call_target="tpu_custom_call", output_to_operand_aliasing={{}: (8, {})} | custom-call | flops 880803840 | bytes 1720320 | tf_op jit(solution)/shard_map/own_project/pallas_call | solution.py:238
  28.1 1.9 %collective-permute-done.9.refs_1_ = bf16[40,1792]{1,0:T(8,128)(2,1)S(1)} collective-permute-done((bf16[40,1792]{1,0:T(8,128)(2,1)S(1)}, bf16[40,1792]{1,0:T(8,128)(2,1)S(1)}, u32[]{:S(2)}, u32[]{:S(2)}) %collective-permute-start.9) | collective-permute-done | bytes 143392 | tf_op jit(solution)/shard_map/ppermute | solution.py:336
  30.0 0.7 %put.2.refs_1_ = bf16[128,3584]{1,0:T(8,128)(2,1)} custom-call(bf16[40,1792]{1,0:T(8,128)(2,1)S(1)} %collective-permute-done.7.refs_0_, bf16[40,1792]{1,0:T(8,128)(2,1)S(1)} %collective-permute-done.9.refs_1_, bf16[128,3584]{1,0:T(8,128)(2,1)} %own_project.3.refs_2_), custom_call_target="tpu_custom_call", output_to_operand_aliasing={{}: (2, {})} | custom-call | bytes 573440 | tf_op jit(solution)/shard_map/put/pallas_call | solution.py:288
  30.7 0.0 collective-permute-done.5.refs_0_
  30.7 0.7 %put.3 = bf16[128,3584]{1,0:T(8,128)(2,1)} custom-call(bf16[48,1792]{1,0:T(8,128)(2,1)S(1)} %collective-permute-done.5.refs_0_, bf16[128,3584]{1,0:T(8,128)(2,1)} %put.2.refs_1_), custom_call_target="tpu_custom_call", output_to_operand_aliasing={{}: (1, {})} | custom-call | bytes 344064 | tf_op jit(solution)/shard_map/put/pallas_call | solution.py:288
  (6 shorter events, 0.0 us)
Async XLA Ops:
  0.0 16.4 %collective-permute-start.4 = (bf16[1024,896]{1,0:T(8,128)(2,1)}, bf16[1024,896]{1,0:T(8,128)(2,1)S(1)}, u32[]{:S(2)}, u32[]{:S(2)}) collective-permute-start(bf16[1024,896]{1,0:T(8,128)(2,1)} %refs_1_.1), channel_id=1, source_target_pairs={{0,1},{1,0},{2,3},{3,2},{4,5},{5,4},{6,7},{7,6},{8,9},{9,8},{10,11... | collective-permute-start | bytes 5505032 | tf_op jit(solution)/shard_map/ppermute | solution.py:336
  0.5 15.9 %collective-permute-start.3 = (bf16[1024,896]{1,0:T(8,128)(2,1)}, bf16[1024,896]{1,0:T(8,128)(2,1)S(1)}, u32[]{:S(2)}, u32[]{:S(2)}) collective-permute-start(bf16[1024,896]{1,0:T(8,128)(2,1)} %refs_0_.1), channel_id=1, source_target_pairs={{0,1},{1,0},{2,3},{3,2},{4,5},{5,4},{6,7},{7,6},{8,9},{9,8},{10,11... | collective-permute-start | bytes 5505032 | tf_op jit(solution)/shard_map/ppermute | solution.py:336
  0.5 15.9 %collective-permute-start.1 = (bf16[128,2,1024]{2,1,0:T(2,128)(2,1)}, bf16[128,2,1024]{2,1,0:T(2,128)(2,1)S(1)}, u32[]{:S(2)}, u32[]{:S(2)}) collective-permute-start(bf16[128,2,1024]{2,1,0:T(2,128)(2,1)} %hidden_ref.1), channel_id=1, source_target_pairs={{0,8},{1,3},{2,10},{3,1},{4,12},{5,7},{6,14},{7,5},{8,0},{9,11},{1... | collective-permute-start | bytes 1572872 | tf_op jit(solution)/shard_map/ppermute | solution.py:344
  4.7 9.3 %collective-permute-start = (bf16[96,1024]{1,0:T(8,128)(2,1)S(1)}, bf16[96,1024]{1,0:T(8,128)(2,1)S(1)}, u32[]{:S(2)}, u32[]{:S(2)}) collective-permute-start(bf16[96,1024]{1,0:T(8,128)(2,1)S(1)} %get-tuple-element.11.refs_2_), channel_id=1, source_target_pairs={{0,2},{1,5},{2,0},{3,7},{4,6},{5,1},{6,4},{7,3},{8,10},{9,13},{10,... | collective-permute-start | bytes 589832 | tf_op jit(solution)/shard_map/ppermute | solution.py:344
  6.3 6.0 %collective-permute-start.2 = (f32[4,128]{1,0:T(4,128)S(1)}, f32[4,128]{1,0:T(4,128)S(1)}, u32[]{:S(2)}, u32[]{:S(2)}) collective-permute-start(f32[4,128]{1,0:T(4,128)S(1)} %get-tuple-element.12.refs_3_), channel_id=1, source_target_pairs={{0,2},{1,3},{2,0},{3,1},{4,6},{5,7},{6,4},{7,5},{8,10},{9,11},{10,... | collective-permute-start | bytes 6152 | tf_op jit(solution)/shard_map/ppermute | solution.py:336
  12.3 7.4 %collective-permute-start.6 = (bf16[80,1024]{1,0:T(8,128)(2,1)S(1)}, bf16[80,1024]{1,0:T(8,128)(2,1)S(1)}, u32[]{:S(2)}, u32[]{:S(2)}) collective-permute-start(bf16[80,1024]{1,0:T(8,128)(2,1)S(1)} %get-tuple-element.15.refs_0_), channel_id=1, source_target_pairs={{0,2},{1,5},{2,0},{3,7},{4,6},{5,1},{6,4},{7,3},{8,10},{9,13},{10,... | collective-permute-start | bytes 491528 | tf_op jit(solution)/shard_map/ppermute | solution.py:344
  14.1 7.4 %collective-permute-start.8 = (bf16[80,1024]{1,0:T(8,128)(2,1)S(1)}, bf16[80,1024]{1,0:T(8,128)(2,1)S(1)}, u32[]{:S(2)}, u32[]{:S(2)}) collective-permute-start(bf16[80,1024]{1,0:T(8,128)(2,1)S(1)} %get-tuple-element.16.refs_1_), channel_id=1, source_target_pairs={{0,2},{1,5},{2,0},{3,7},{4,6},{5,1},{6,4},{7,3},{8,10},{9,13},{10,... | collective-permute-start | bytes 491528 | tf_op jit(solution)/shard_map/ppermute | solution.py:344
  17.9 12.8 %collective-permute-start.5 = (bf16[48,1792]{1,0:T(8,128)(2,1)S(1)}, bf16[48,1792]{1,0:T(8,128)(2,1)S(1)}, u32[]{:S(2)}, u32[]{:S(2)}) collective-permute-start(bf16[48,1792]{1,0:T(8,128)(2,1)S(1)} %far_project.3), channel_id=1, source_target_pairs={{0,2},{1,3},{2,0},{3,1},{4,6},{5,7},{6,4},{7,5},{8,10},{9,11},{10,... | collective-permute-start | bytes 516104 | tf_op jit(solution)/shard_map/ppermute | solution.py:336
  21.2 6.9 %collective-permute-start.7 = (bf16[40,1792]{1,0:T(8,128)(2,1)S(1)}, bf16[40,1792]{1,0:T(8,128)(2,1)S(1)}, u32[]{:S(2)}, u32[]{:S(2)}) collective-permute-start(bf16[40,1792]{1,0:T(8,128)(2,1)S(1)} %far_project.4), channel_id=1, source_target_pairs={{0,2},{1,3},{2,0},{3,1},{4,6},{5,7},{6,4},{7,5},{8,10},{9,11},{10,... | collective-permute-start | bytes 430088 | tf_op jit(solution)/shard_map/ppermute | solution.py:336
  22.9 7.0 %collective-permute-start.9 = (bf16[40,1792]{1,0:T(8,128)(2,1)S(1)}, bf16[40,1792]{1,0:T(8,128)(2,1)S(1)}, u32[]{:S(2)}, u32[]{:S(2)}) collective-permute-start(bf16[40,1792]{1,0:T(8,128)(2,1)S(1)} %far_project.5), channel_id=1, source_target_pairs={{0,2},{1,3},{2,0},{3,1},{4,6},{5,7},{6,4},{7,5},{8,10},{9,11},{10,... | collective-permute-start | bytes 430088 | tf_op jit(solution)/shard_map/ppermute | solution.py:336

commit v6 on v5

--- a/solution.py
+++ b/solution.py
@@ -10,7 +10,7 @@
 VMEM = pl.BlockSpec(memory_space=pltpu.VMEM)
 ANY = pl.BlockSpec(memory_space=pl.ANY)
 SLAB = 128
-CUTS = (0, 5, 10, 16)
+CUTS = (0, 5, 12, 16)
 
 
 def general_body(expert_ids, gate_weights, hidden, hot_down, cold_down):
@@ -337,7 +337,7 @@
 
     def send_by(array, core):
         pairs = [
-            (g * devices + i, g * devices + (i ^ 2) if i % 2 == core else (g ^ (1 + core)) * devices + i)
+            (g * devices + i, g * devices + (i ^ 2) if i % 2 == core else (g ^ (2 - core)) * devices + i)
             for g in range(groups)
             for i in range(devices)
         ]
@@ -353,10 +353,10 @@
     back = []
     for i, (a, b) in enumerate(spans):
         if i == 2:
-            out = own_project(((0, (1,)),), held, gates, own, out)
+            out = own_project(((0, (1,)), (1, (1,))), held, gates, (*own, *partner), out)
         result = far_project(a, b - a, moved[i], whole, far_gates, own, partner)
         back.append(send(result, far))
-    out = own_project(((0, (0,)), (1, (0, 1))), held, gates, (*own, *partner), out)
+    out = own_project(((0, (0,)), (1, (0,))), held, gates, (*own, *partner), out)
     starts = [a for a, _ in spans]
     out = put(starts[:-1], back[:-1], out)
     out = put(starts[-1:], back[-1:], out)

time: 31.6 us -> 31.7 us (level)
  no operation moved by 1% of the time
where the time goes in v6:
time: 31.7 us; the launch traced here: 31.6 us
  Pallas kernels  12.4 us (39%)
  starting transfers between devices  11.6 us (37%)
  waiting for transfers between devices  7.51 us (24%)
    ppermute x6, waiting for transfers between devices, send(): return lax.ppermute(array, 'expert', pairs)  7.5 us
    ppermute x4, starting transfers between devices, send_by(): return lax.ppermute(array, ('dp', 'expert'), pairs)  6.58 us
    ppermute x6, starting transfers between devices, send(): return lax.ppermute(array, 'expert', pairs)  5.01 us
    pallas_call x3, Pallas kernels, far_project(): pl.pallas_call(functools.partial(far_kernel, start), name='far_project',...  4.34 us
    pallas_call x2, Pallas kernels, own_project(): pl.pallas_call(functools.partial(own_kernel, blocks, len(rows)), name='ow...  3.36 us
    pallas_call x1, Pallas kernels, hold(): pl.pallas_call(hold_kernel, name='hold', out_shape=[pltpu.VMEM(a.shape, a...  2.07 us
    pallas_call x2, Pallas kernels, put(): pl.pallas_call(functools.partial(put_kernel, starts), name='put', out_sha...  1.43 us
    pallas_call x1, Pallas kernels, take(): pl.pallas_call(take_kernel, name='take', out_shape=shapes, in_specs=[ANY]...  1.17 us
  transfers between devices with their start and end apart: 10, of which 2 were waited for; matrix products, arithmetic and copies ran while one was open for 0% of the time, Pallas kernels for 37%

profile of v6, /device:TPU:0, one launch (start us, length us, event | category | flops | bytes accessed | tf_op | source)
XLA Modules:
  0.0 31.6 jit_solution(5882957938763142217)
XLA Ops:
  0.0 0.5 %collective-permute-start.4 = (bf16[1024,896]{1,0:T(8,128)(2,1)}, bf16[1024,896]{1,0:T(8,128)(2,1)S(1)}, u32[]{:S(2)}, u32[]{:S(2)}) collective-permute-start(bf16[1024,896]{1,0:T(8,128)(2,1)} %refs_1_.1), channel_id=1, source_target_pairs={{0,1},{1,0},{2,3},{3,2},{4,5},{5,4},{6,7},{7,6},{8,9},{9,8},{10,11... | collective-permute-start | bytes 5505032 | tf_op jit(solution)/shard_map/ppermute | solution.py:336
  0.5 0.0 collective-permute-start.3
  0.5 3.0 %collective-permute-start.1 = (bf16[128,2,1024]{2,1,0:T(2,128)(2,1)}, bf16[128,2,1024]{2,1,0:T(2,128)(2,1)S(1)}, u32[]{:S(2)}, u32[]{:S(2)}) collective-permute-start(bf16[128,2,1024]{2,1,0:T(2,128)(2,1)} %hidden_ref.1), channel_id=1, source_target_pairs={{0,4},{1,3},{2,6},{3,1},{4,0},{5,7},{6,2},{7,5},{8,12},{9,11},{10,... | collective-permute-start | bytes 1572872 | tf_op jit(solution)/shard_map/ppermute | solution.py:344
  3.5 1.2 %take.1 = (bf16[80,1024]{1,0:T(8,128)(2,1)S(1)}, bf16[112,1024]{1,0:T(8,128)(2,1)S(1)}, bf16[64,1024]{1,0:T(8,128)(2,1)S(1)}, f32[4,128]{1,0:T(4,128)S(1)}) custom-call(bf16[128,2,1024]{2,1,0:T(2,128)(2,1)} %hidden_ref.1, s32[2,128]{1,0:T(2,128)} %bitcast.2, f32[2,128]{1,0:T(2,128)} %bitcast.3), custom_call_target="tpu_custom_call" | custom-call | bytes 1048576 | tf_op jit(solution)/shard_map/take/pallas_call | solution.py:111
  4.7 1.6 %collective-permute-start.8 = (bf16[112,1024]{1,0:T(8,128)(2,1)S(1)}, bf16[112,1024]{1,0:T(8,128)(2,1)S(1)}, u32[]{:S(2)}, u32[]{:S(2)}) collective-permute-start(bf16[112,1024]{1,0:T(8,128)(2,1)S(1)} %get-tuple-element.16.refs_1_), channel_id=1, source_target_pairs={{0,2},{1,9},{2,0},{3,11},{4,6},{5,13},{6,4},{7,15},{8,10},{9,1},{1... | collective-permute-start | bytes 688136 | tf_op jit(solution)/shard_map/ppermute | solution.py:344
  6.2 0.5 %collective-permute-start.2 = (f32[4,128]{1,0:T(4,128)S(1)}, f32[4,128]{1,0:T(4,128)S(1)}, u32[]{:S(2)}, u32[]{:S(2)}) collective-permute-start(f32[4,128]{1,0:T(4,128)S(1)} %get-tuple-element.12.refs_3_), channel_id=1, source_target_pairs={{0,2},{1,3},{2,0},{3,1},{4,6},{5,7},{6,4},{7,5},{8,10},{9,11},{10,... | collective-permute-start | bytes 6152 | tf_op jit(solution)/shard_map/ppermute | solution.py:336
  6.8 5.9 %collective-permute-done.2.gates_ref = f32[4,128]{1,0:T(4,128)S(1)} collective-permute-done((f32[4,128]{1,0:T(4,128)S(1)}, f32[4,128]{1,0:T(4,128)S(1)}, u32[]{:S(2)}, u32[]{:S(2)}) %collective-permute-start.2) | collective-permute-done | bytes 2080 | tf_op jit(solution)/shard_map/ppermute | solution.py:336
  12.7 1.7 %collective-permute-start.6 = (bf16[80,1024]{1,0:T(8,128)(2,1)S(1)}, bf16[80,1024]{1,0:T(8,128)(2,1)S(1)}, u32[]{:S(2)}, u32[]{:S(2)}) collective-permute-start(bf16[80,1024]{1,0:T(8,128)(2,1)S(1)} %get-tuple-element.15.refs_0_), channel_id=1, source_target_pairs={{0,2},{1,9},{2,0},{3,11},{4,6},{5,13},{6,4},{7,15},{8,10},{9,1},{1... | collective-permute-start | bytes 491528 | tf_op jit(solution)/shard_map/ppermute | solution.py:344
  14.4 0.0 collective-permute-done.8.part_ref
  14.4 0.3 collective-permute-start
  14.7 2.1 %hold.1 = (bf16[1024,896]{1,0:T(8,128)(2,1)S(1)}, bf16[1024,896]{1,0:T(8,128)(2,1)S(1)}) custom-call(bf16[1024,896]{1,0:T(8,128)(2,1)} %refs_0_.1, bf16[1024,896]{1,0:T(8,128)(2,1)} %refs_1_.1), custom_call_target="tpu_custom_call" | custom-call | bytes 7340032 | tf_op jit(solution)/shard_map/hold/pallas_call | solution.py:313
  16.8 0.0 collective-permute-done.1.whole_ref
  16.8 0.0 collective-permute-done.3.c1.refs_6_
  16.8 1.5 %far_project.5 = bf16[56,1792]{1,0:T(8,128)(2,1)S(1)} custom-call(bf16[112,1024]{1,0:T(8,128)(2,1)S(1)} %collective-permute-done.8.part_ref, bf16[128,2,1024]{2,1,0:T(2,128)(2,1)S(1)} %collective-permute-done.1.whole_ref, f32[4,128]{1,0:T(4,128)S(1)} %collective-permute-done.2.gates_ref, bf16[1024,896]{1,0:T(8,128)(2,1)S(1)} %get-tuple-element.13.c0.refs_4_, ...), custom_call_target="tpu_custom_call" | custom-call | flops 411041792 | bytes 802816 | tf_op jit(solution)/shard_map/far_project/pallas_call | solution.py:184
  18.3 1.8 %collective-permute-start.9 = (bf16[56,1792]{1,0:T(8,128)(2,1)S(1)}, bf16[56,1792]{1,0:T(8,128)(2,1)S(1)}, u32[]{:S(2)}, u32[]{:S(2)}) collective-permute-start(bf16[56,1792]{1,0:T(8,128)(2,1)S(1)} %far_project.5), channel_id=1, source_target_pairs={{0,2},{1,3},{2,0},{3,1},{4,6},{5,7},{6,4},{7,5},{8,10},{9,11},{10,... | collective-permute-start | bytes 602120 | tf_op jit(solution)/shard_map/ppermute | solution.py:336
  20.1 1.4 %far_project.3 = bf16[32,1792]{1,0:T(8,128)(2,1)S(1)} custom-call(bf16[64,1024]{1,0:T(8,128)(2,1)S(1)} %collective-permute-done.part_ref, bf16[128,2,1024]{2,1,0:T(2,128)(2,1)S(1)} %collective-permute-done.1.whole_ref, f32[4,128]{1,0:T(4,128)S(1)} %collective-permute-done.2.gates_ref, bf16[1024,896]{1,0:T(8,128)(2,1)S(1)} %get-tuple-element.13.c0.refs_4_, ...), custom_call_target="tpu_custom_call" | custom-call | flops 234881024 | bytes 458752 | tf_op jit(solution)/shard_map/far_project/pallas_call | solution.py:184
  21.5 1.1 %collective-permute-start.5 = (bf16[32,1792]{1,0:T(8,128)(2,1)S(1)}, bf16[32,1792]{1,0:T(8,128)(2,1)S(1)}, u32[]{:S(2)}, u32[]{:S(2)}) collective-permute-start(bf16[32,1792]{1,0:T(8,128)(2,1)S(1)} %far_project.3), channel_id=1, source_target_pairs={{0,2},{1,3},{2,0},{3,1},{4,6},{5,7},{6,4},{7,5},{8,10},{9,11},{10,... | collective-permute-start | bytes 344072 | tf_op jit(solution)/shard_map/ppermute | solution.py:336
  22.6 0.0 collective-permute-done.6.part_ref
  22.6 1.4 %far_project.4 = bf16[40,1792]{1,0:T(8,128)(2,1)S(1)} custom-call(bf16[80,1024]{1,0:T(8,128)(2,1)S(1)} %collective-permute-done.6.part_ref, bf16[128,2,1024]{2,1,0:T(2,128)(2,1)S(1)} %collective-permute-done.1.whole_ref, f32[4,128]{1,0:T(4,128)S(1)} %collective-permute-done.2.gates_ref, bf16[1024,896]{1,0:T(8,128)(2,1)S(1)} %get-tuple-element.13.c0.refs_4_, ...), custom_call_target="tpu_custom_call" | custom-call | flops 293601280 | bytes 573440 | tf_op jit(solution)/shard_map/far_project/pallas_call | solution.py:184
  24.0 1.1 %collective-permute-start.7 = (bf16[40,1792]{1,0:T(8,128)(2,1)S(1)}, bf16[40,1792]{1,0:T(8,128)(2,1)S(1)}, u32[]{:S(2)}, u32[]{:S(2)}) collective-permute-start(bf16[40,1792]{1,0:T(8,128)(2,1)S(1)} %far_project.4), channel_id=1, source_target_pairs={{0,2},{1,3},{2,0},{3,1},{4,6},{5,7},{6,4},{7,5},{8,10},{9,11},{10,... | collective-permute-start | bytes 430088 | tf_op jit(solution)/shard_map/ppermute | solution.py:336
  25.2 3.3 %own_project.3.refs_2_ = bf16[128,3584]{1,0:T(8,128)(2,1)} custom-call(bf16[80,1024]{1,0:T(8,128)(2,1)S(1)} %get-tuple-element.15.refs_0_, bf16[112,1024]{1,0:T(8,128)(2,1)S(1)} %get-tuple-element.16.refs_1_, bf16[64,1024]{1,0:T(8,128)(2,1)S(1)} %get-tuple-element.11.refs_2_, ...), custom_call_target="tpu_custom_call", output_to_operand_aliasing={{}: (8, {})} | custom-call | flops 880803840 | bytes 1720320 | tf_op jit(solution)/shard_map/own_project/pallas_call | solution.py:238
  28.5 1.6 %collective-permute-done.7.refs_0_ = bf16[40,1792]{1,0:T(8,128)(2,1)S(1)} collective-permute-done((bf16[40,1792]{1,0:T(8,128)(2,1)S(1)}, bf16[40,1792]{1,0:T(8,128)(2,1)S(1)}, u32[]{:S(2)}, u32[]{:S(2)}) %collective-permute-start.7) | collective-permute-done | bytes 143392 | tf_op jit(solution)/shard_map/ppermute | solution.py:336
  30.1 0.8 %put.2.refs_1_ = bf16[128,3584]{1,0:T(8,128)(2,1)} custom-call(bf16[40,1792]{1,0:T(8,128)(2,1)S(1)} %collective-permute-done.7.refs_0_, bf16[56,1792]{1,0:T(8,128)(2,1)S(1)} %collective-permute-done.9.refs_1_, bf16[128,3584]{1,0:T(8,128)(2,1)} %own_project.3.refs_2_), custom_call_target="tpu_custom_call", output_to_operand_aliasing={{}: (2, {})} | custom-call | bytes 688128 | tf_op jit(solution)/shard_map/put/pallas_call | solution.py:288
  30.9 0.7 %put.3 = bf16[128,3584]{1,0:T(8,128)(2,1)} custom-call(bf16[32,1792]{1,0:T(8,128)(2,1)S(1)} %collective-permute-done.5.refs_0_, bf16[128,3584]{1,0:T(8,128)(2,1)} %put.2.refs_1_), custom_call_target="tpu_custom_call", output_to_operand_aliasing={{}: (1, {})} | custom-call | bytes 229376 | tf_op jit(solution)/shard_map/put/pallas_call | solution.py:288
  (6 shorter events, 0.0 us)
Async XLA Ops:
  0.0 16.8 %collective-permute-start.4 = (bf16[1024,896]{1,0:T(8,128)(2,1)}, bf16[1024,896]{1,0:T(8,128)(2,1)S(1)}, u32[]{:S(2)}, u32[]{:S(2)}) collective-permute-start(bf16[1024,896]{1,0:T(8,128)(2,1)} %refs_1_.1), channel_id=1, source_target_pairs={{0,1},{1,0},{2,3},{3,2},{4,5},{5,4},{6,7},{7,6},{8,9},{9,8},{10,11... | collective-permute-start | bytes 5505032 | tf_op jit(solution)/shard_map/ppermute | solution.py:336
  0.5 16.3 %collective-permute-start.3 = (bf16[1024,896]{1,0:T(8,128)(2,1)}, bf16[1024,896]{1,0:T(8,128)(2,1)S(1)}, u32[]{:S(2)}, u32[]{:S(2)}) collective-permute-start(bf16[1024,896]{1,0:T(8,128)(2,1)} %refs_0_.1), channel_id=1, source_target_pairs={{0,1},{1,0},{2,3},{3,2},{4,5},{5,4},{6,7},{7,6},{8,9},{9,8},{10,11... | collective-permute-start | bytes 5505032 | tf_op jit(solution)/shard_map/ppermute | solution.py:336
  0.5 16.3 %collective-permute-start.1 = (bf16[128,2,1024]{2,1,0:T(2,128)(2,1)}, bf16[128,2,1024]{2,1,0:T(2,128)(2,1)S(1)}, u32[]{:S(2)}, u32[]{:S(2)}) collective-permute-start(bf16[128,2,1024]{2,1,0:T(2,128)(2,1)} %hidden_ref.1), channel_id=1, source_target_pairs={{0,4},{1,3},{2,6},{3,1},{4,0},{5,7},{6,2},{7,5},{8,12},{9,11},{10,... | collective-permute-start | bytes 1572872 | tf_op jit(solution)/shard_map/ppermute | solution.py:344
  4.7 9.7 %collective-permute-start.8 = (bf16[112,1024]{1,0:T(8,128)(2,1)S(1)}, bf16[112,1024]{1,0:T(8,128)(2,1)S(1)}, u32[]{:S(2)}, u32[]{:S(2)}) collective-permute-start(bf16[112,1024]{1,0:T(8,128)(2,1)S(1)} %get-tuple-element.16.refs_1_), channel_id=1, source_target_pairs={{0,2},{1,9},{2,0},{3,11},{4,6},{5,13},{6,4},{7,15},{8,10},{9,1},{1... | collective-permute-start | bytes 688136 | tf_op jit(solution)/shard_map/ppermute | solution.py:344
  6.2 6.4 %collective-permute-start.2 = (f32[4,128]{1,0:T(4,128)S(1)}, f32[4,128]{1,0:T(4,128)S(1)}, u32[]{:S(2)}, u32[]{:S(2)}) collective-permute-start(f32[4,128]{1,0:T(4,128)S(1)} %get-tuple-element.12.refs_3_), channel_id=1, source_target_pairs={{0,2},{1,3},{2,0},{3,1},{4,6},{5,7},{6,4},{7,5},{8,10},{9,11},{10,... | collective-permute-start | bytes 6152 | tf_op jit(solution)/shard_map/ppermute | solution.py:336
  12.7 9.9 %collective-permute-start.6 = (bf16[80,1024]{1,0:T(8,128)(2,1)S(1)}, bf16[80,1024]{1,0:T(8,128)(2,1)S(1)}, u32[]{:S(2)}, u32[]{:S(2)}) collective-permute-start(bf16[80,1024]{1,0:T(8,128)(2,1)S(1)} %get-tuple-element.15.refs_0_), channel_id=1, source_target_pairs={{0,2},{1,9},{2,0},{3,11},{4,6},{5,13},{6,4},{7,15},{8,10},{9,1},{1... | collective-permute-start | bytes 491528 | tf_op jit(solution)/shard_map/ppermute | solution.py:344
  14.4 5.7 %collective-permute-start = (bf16[64,1024]{1,0:T(8,128)(2,1)S(1)}, bf16[64,1024]{1,0:T(8,128)(2,1)S(1)}, u32[]{:S(2)}, u32[]{:S(2)}) collective-permute-start(bf16[64,1024]{1,0:T(8,128)(2,1)S(1)} %get-tuple-element.11.refs_2_), channel_id=1, source_target_pairs={{0,2},{1,9},{2,0},{3,11},{4,6},{5,13},{6,4},{7,15},{8,10},{9,1},{1... | collective-permute-start | bytes 393224 | tf_op jit(solution)/shard_map/ppermute | solution.py:344
  18.3 11.8 %collective-permute-start.9 = (bf16[56,1792]{1,0:T(8,128)(2,1)S(1)}, bf16[56,1792]{1,0:T(8,128)(2,1)S(1)}, u32[]{:S(2)}, u32[]{:S(2)}) collective-permute-start(bf16[56,1792]{1,0:T(8,128)(2,1)S(1)} %far_project.5), channel_id=1, source_target_pairs={{0,2},{1,3},{2,0},{3,1},{4,6},{5,7},{6,4},{7,5},{8,10},{9,11},{10,... | collective-permute-start | bytes 602120 | tf_op jit(solution)/shard_map/ppermute | solution.py:336
  21.5 9.3 %collective-permute-start.5 = (bf16[32,1792]{1,0:T(8,128)(2,1)S(1)}, bf16[32,1792]{1,0:T(8,128)(2,1)S(1)}, u32[]{:S(2)}, u32[]{:S(2)}) collective-permute-start(bf16[32,1792]{1,0:T(8,128)(2,1)S(1)} %far_project.3), channel_id=1, source_target_pairs={{0,2},{1,3},{2,0},{3,1},{4,6},{5,7},{6,4},{7,5},{8,10},{9,11},{10,... | collective-permute-start | bytes 344072 | tf_op jit(solution)/shard_map/ppermute | solution.py:336
  24.0 6.1 %collective-permute-start.7 = (bf16[40,1792]{1,0:T(8,128)(2,1)S(1)}, bf16[40,1792]{1,0:T(8,128)(2,1)S(1)}, u32[]{:S(2)}, u32[]{:S(2)}) collective-permute-start(bf16[40,1792]{1,0:T(8,128)(2,1)S(1)} %far_project.4), channel_id=1, source_target_pairs={{0,2},{1,3},{2,0},{3,1},{4,6},{5,7},{6,4},{7,5},{8,10},{9,11},{10,... | collective-permute-start | bytes 430088 | tf_op jit(solution)/shard_map/ppermute | solution.py:336
